TPU v7x, 256 devices: a whole 4x4x8 slice. The times are simulated.
256 devices in a mesh: grp: 2 (over core), dev: 128 (over x, y, z).
Axes of the slice: x: 4, y: 4, z: 8, core: 2. Of those that a mesh axis runs over, the one named last changes fastest.
Arguments:
- coarse_emb: bfloat16 [131072, 128], P('dev'), may hold values from -6 to 6
- req_ids: int32 [128, 2, 128, 16], P('dev', 'grp'), may hold values from 0 to 1023, as said below
- fine_slot: int32 [128, 2, 2048], P('dev', 'grp'), may hold values from 0 to 2047, as said below
- tiles: bfloat16 [4096, 2, 8, 128, 128], P('dev', 'grp'), may hold values from -0.125 to 0.125
- tile_cols: int32 [4096, 2, 8], P('dev', 'grp'), may hold values from 0 to 47
Outputs:
- smoothed: bfloat16 [524288, 128], P('dev')
Inputs may be any that keep to these rules, and one draw needn't show every extreme that they name: For each d, g and o only the first entries of req_ids[d, g, o] are requested, at most 16 of them, and for each d and g some owner o has all 16; the remaining entries are 0. fine_slot[d, g, i] = o * 16 + j always names a requested entry j of req_ids[d, g, o], and every requested entry is named by some fine node.
All inputs are finite; a program needn't handle non-finite values.
Results may differ from a plain program's by a relative error of at most 0.001.
Values may be sent and summed in bfloat16 or wider, within the bound.
No kernel may reach another device: no remote copies, remote signals or barrier semaphores. Data moves between devices by JAX's collectives and lax.ppermute only.
A program may use at most 64 MiB of HBM per device.

v0:
```python
import jax
import jax.numpy as jnp
from jax import lax
from jax.sharding import PartitionSpec as P


def with_halo(shard, sides, width):
    for axis, dim in sides:
        count, length = (lax.axis_size(axis), shard.shape[dim])
        up = [(i, (i + 1) % count) for i in range(count - 1)]
        down = [(j, i) for i, j in up]
        last = lax.slice_in_dim(shard, length - width, length, axis=dim)
        initial = lax.slice_in_dim(shard, 0, width, axis=dim)
        before = lax.ppermute(last, axis, up)
        after = lax.ppermute(initial, axis, down)
        shard = jnp.concatenate([before, shard, after], axis=dim)
    return shard


def per_device(coarse_emb, req_ids, fine_slot, tiles, tile_cols):
    owners = lax.axis_size("dev")
    slot_count = req_ids.shape[3]
    feature_dim = coarse_emb.shape[1]
    half_rows = fine_slot.shape[2]
    tile_rows = tiles.shape[3]
    fine_rows = tiles.shape[0] * tile_rows
    wanted_rows = jnp.take(
        coarse_emb, lax.all_to_all(req_ids, "dev", split_axis=2, concat_axis=0, tiled=True), axis=0
    )
    received = lax.all_to_all(wanted_rows, "dev", split_axis=0, concat_axis=2, tiled=True)
    slot_table = received.reshape(owners * slot_count, feature_dim)
    rows_per = min(512, half_rows)
    block_count = half_rows // rows_per
    columns = lax.iota(jnp.int32, owners * slot_count)

    def lift_block(slot_block):
        onehot = (slot_block[:, None] == columns[None, :]).astype(jnp.bfloat16)
        return jnp.dot(onehot, slot_table, preferred_element_type=jnp.float32).astype(jnp.bfloat16)

    lifted = lax.map(lift_block, fine_slot.reshape(block_count, rows_per)).reshape(
        half_rows, feature_dim
    )
    extended = with_halo(lifted, (("dev", 0),), half_rows)
    ext_blocks = extended.reshape(3 * half_rows // tile_rows, tile_rows, feature_dim)
    picked = ext_blocks[tile_cols[:, 0, :]]
    tile_sums = jnp.einsum(
        "rtij,rtjw->riw", tiles[:, 0], picked, preferred_element_type=jnp.float32
    )
    tile_sums = tile_sums.reshape(fine_rows, feature_dim)
    group = lax.axis_index("grp")
    own_part = lax.dynamic_update_slice(
        jnp.zeros((fine_rows, feature_dim), jnp.float32),
        lifted.astype(jnp.float32),
        (group * half_rows, 0),
    )
    partial_value = own_part - 0.5 * tile_sums
    summed = lax.psum(partial_value, "grp")
    return summed.astype(jnp.bfloat16)


def solution(mesh):
    return jax.shard_map(
        per_device,
        mesh=mesh,
        in_specs=(
            P("dev", None),
            P("dev", "grp", None, None),
            P("dev", "grp", None),
            P("dev", "grp", None, None, None),
            P("dev", "grp", None),
        ),
        out_specs=P("dev", None),
        check_vma=False,
    )
```

profile of v0, /device:TPU:1, one launch (start us, length us, event | category | flops | bytes accessed | tf_op | source)
XLA Modules:
  0.0 108.3 jit_solution(4448812067448210851)
XLA Ops:
  0.0 0.0 copy-start
  0.0 0.8 copy.10
  0.8 26.7 %all_to_all.24 = s32[1,1,128,16]{3,1,0,2:T(1,128)S(1)} all-to-all(s32[1,1,128,16]{3,1,0,2:T(1,128)S(1)} %copy.10), channel_id=1, replica_groups=mesh['grp'=2,'dev'=128] {'dev'}, dimensions={2} | all-to-all | bytes 16384 | tf_op jit(solution)/shard_map/all_to_all | solution.py:28
  27.6 0.1 reshape.137
  27.7 0.0 copy-done
  27.7 0.0 copy-start.3
  27.7 0.0 copy-start.4
  27.7 6.2 %gather_fusion = bf16[2048,128]{1,0:T(8,128)(2,1)S(1)} fusion(bf16[1024,128]{1,0:T(8,128)(2,1)S(1)} %copy-done, s32[2048]{0:T(1024)S(1)} %broadcast_clamp_fusion), kind=kCustom, calls=%fused_computation | custom fusion | bytes 1056768 | tf_op jit(solution)/shard_map/jit(_take)/gather | solution.py:27
  33.9 1.1 %broadcast_select_fusion = bf16[128,1,1,16,128]{4,3,2,1,0:T(8,128)(2,1)} fusion(bf16[128,1,1,16,128]{4,3,2,1,0:T(8,128)(2,1)S(1)} %bitcast.44, pred[128,16]{1,0:T(8,128)(4,1)S(1)} %compare_and_fusion), kind=kLoop, calls=%fused_computation.16 | loop fusion | flops 262144 | bytes 1050624 | tf_op jit(solution)/shard_map/jit(_take)/select_n | solution.py:27
  35.0 6.2 %all-to-all-start.1 = ((bf16[128,1,1,16,128]{4,3,2,1,0:T(8,128)(2,1)}), bf16[128,1,1,16,128]{4,3,2,1,0:T(8,128)(2,1)S(1)}, u32[]{:S(2)}, u32[]{:S(2)}) async-start(bf16[128,1,1,16,128]{4,3,2,1,0:T(8,128)(2,1)} %broadcast_select_fusion), calls=%async_computation.1 | async-start | bytes 1048576 | tf_op jit(solution)/shard_map/all_to_all | solution.py:30
  41.2 0.5 broadcast.89
  41.8 0.6 reduce.3
  42.4 0.0 copy-done.4
  42.4 0.1 copy.12
  42.5 0.1 reshape.145
  42.5 17.0 %all-to-all-done.1 = bf16[128,1,1,16,128]{4,3,2,1,0:T(8,128)(2,1)S(1)} async-done(((bf16[128,1,1,16,128]{4,3,2,1,0:T(8,128)(2,1)}), bf16[128,1,1,16,128]{4,3,2,1,0:T(8,128)(2,1)S(1)}, u32[]{:S(2)}, u32[]{:S(2)}) %all-to-all-start.1) | async-done | bytes 524320 | tf_op jit(solution)/shard_map/all_to_all | solution.py:30
  59.5 3.7 %while.11 = (s32[]{:T(128)}, bf16[4,512,128]{2,1,0:T(8,128)(2,1)S(1)}, s32[4,512]{1,0:T(4,128)S(1)}, bf16[2048,128]{1,0:T(8,128)(2,1)S(1)}, s32[]{:T(128)}) while((s32[]{:T(128)}, bf16[4,512,128]{2,1,0:T(8,128)(2,1)S(1)}, s32[4,512]{1,0:T(4,128)S(1)}, bf16[2048,128]{1,0:T(8,128)(2,1)S(1)}, s32[]{:T(128)}) %tuple.24), condition=%wide.region_1.2_spmd.clone, body=%wide.region_0.1_spmd.clone.sunk | while | flops 269549568 | bytes 661573 | solution.py:40
  59.5 0.9 fusion.16
  60.4 0.9 fusion.16
  61.4 0.9 fusion.16
  62.3 0.9 fusion.16
  63.2 2.5 %collective-permute-start = (bf16[2048,128]{1,0:T(8,128)(2,1)S(1)}, bf16[2048,128]{1,0:T(8,128)(2,1)S(1)}, u32[]{:S(2)}, u32[]{:S(2)}) collective-permute-start(bf16[2048,128]{1,0:T(8,128)(2,1)S(1)} %bitcast.45), channel_id=1, source_target_pairs={{0,1},{1,2},{2,3},{3,4},{4,5},{5,6},{6,7},{7,8},{8,9},{9,10},{10,1... | collective-permute-start | bytes 1572872 | tf_op jit(solution)/shard_map/ppermute | solution.py:14
  65.7 1.3 %collective-permute-start.1 = (bf16[2048,128]{1,0:T(8,128)(2,1)S(1)}, bf16[2048,128]{1,0:T(8,128)(2,1)S(1)}, u32[]{:S(2)}, u32[]{:S(2)}) collective-permute-start(bf16[2048,128]{1,0:T(8,128)(2,1)S(1)} %bitcast.46), channel_id=1, source_target_pairs={{1,0},{2,1},{3,2},{4,3},{5,4},{6,5},{7,6},{8,7},{9,8},{10,9},{11,1... | collective-permute-start | bytes 1572872 | tf_op jit(solution)/shard_map/ppermute | solution.py:15
  67.0 0.1 broadcast_in_dim.23
  67.2 0.1 convert_dynamic-update-slice_fusion
  67.3 6.6 %collective-permute-done = bf16[2048,128]{1,0:T(8,128)(2,1)S(1)} collective-permute-done((bf16[2048,128]{1,0:T(8,128)(2,1)S(1)}, bf16[2048,128]{1,0:T(8,128)(2,1)S(1)}, u32[]{:S(2)}, u32[]{:S(2)}) %collective-permute-start) | collective-permute-done | bytes 524320 | tf_op jit(solution)/shard_map/ppermute | solution.py:14
  73.8 3.9 %collective-permute-done.1 = bf16[2048,128]{1,0:T(8,128)(2,1)S(1)} collective-permute-done((bf16[2048,128]{1,0:T(8,128)(2,1)S(1)}, bf16[2048,128]{1,0:T(8,128)(2,1)S(1)}, u32[]{:S(2)}, u32[]{:S(2)}) %collective-permute-start.1) | collective-permute-done | bytes 524320 | tf_op jit(solution)/shard_map/ppermute | solution.py:15
  77.7 0.1 pad_maximum_fusion
  77.8 8.6 %gather_fusion.1 = bf16[256,128,128]{2,1,0:T(8,128)(2,1)} fusion(bf16[48,128,128]{2,1,0:T(8,128)(2,1)S(1)} %bitcast.42, s32[1024]{0:T(1024)S(1)} %pad_clamp_fusion), kind=kCustom, calls=%fused_computation.1 | custom fusion | bytes 16778240 | tf_op jit(solution)/shard_map/gather | solution.py:45
  86.4 8.3 %bitcast_multiply_fusion = f32[32,128,128]{1,2,0:T(8,128)S(1)} fusion(bf16[32,8,128,128]{3,2,1,0:T(8,128)(2,1)} %bitcast.43, bf16[32,1,8,128,128]{4,3,2,1,0:T(8,128)(2,1)} %param.10), kind=kOutput, calls=%fused_computation.13 | convolution fusion | flops 1074266112 | bytes 18874368 | tf_op jit(solution)/shard_map/rtij,rtjw->riw/dot_general | solution.py:46
  94.7 0.2 bitcast_subtract_fusion
  94.9 13.4 %all-reduce.1 = bf16[4096,128]{1,0:T(8,128)(2,1)} all-reduce(f32[4096,128]{1,0:T(8,128)S(1)} %bitcast_subtract_fusion), channel_id=1, replica_groups=mesh['grp'=2,'dev'=128] {'grp'}, use_global_device_ids=true, to_apply=%region_2.3 | all-reduce | flops 524288 | bytes 3145728 | tf_op jit(solution)/shard_map/psum | solution.py:57
  (16 shorter events, 0.1 us)
Async XLA Ops:
  0.0 27.7 %copy-start = (bf16[1024,128]{1,0:T(8,128)(2,1)S(1)}, bf16[1024,128]{1,0:T(8,128)(2,1)}, u32[]{:S(2)}) copy-start(bf16[1024,128]{1,0:T(8,128)(2,1)} %param.7) | copy-start | bytes 786436
  27.7 14.1 %copy-start.3 = (s32[1,1,2048]{2,1,0:T(1,128)S(1)}, s32[1,1,2048]{2,1,0:T(1,128)}, u32[]{:S(2)}) copy-start(s32[1,1,2048]{2,1,0:T(1,128)} %param.9) | copy-start | bytes 24580
  27.7 14.6 %copy-start.4 = (s32[32,1,8]{0,2,1:T(8,128)S(1)}, s32[32,1,8]{0,2,1:T(8,128)}, u32[]{:S(2)}) copy-start(s32[32,1,8]{0,2,1:T(8,128)} %param.11) | copy-start | bytes 3076
  35.0 24.5 %all-to-all-start.1 = ((bf16[128,1,1,16,128]{4,3,2,1,0:T(8,128)(2,1)}), bf16[128,1,1,16,128]{4,3,2,1,0:T(8,128)(2,1)S(1)}, u32[]{:S(2)}, u32[]{:S(2)}) async-start(bf16[128,1,1,16,128]{4,3,2,1,0:T(8,128)(2,1)} %broadcast_select_fusion), calls=%async_computation.1 | async-start | bytes 1048576 | tf_op jit(solution)/shard_map/all_to_all | solution.py:30
  63.2 10.6 %collective-permute-start = (bf16[2048,128]{1,0:T(8,128)(2,1)S(1)}, bf16[2048,128]{1,0:T(8,128)(2,1)S(1)}, u32[]{:S(2)}, u32[]{:S(2)}) collective-permute-start(bf16[2048,128]{1,0:T(8,128)(2,1)S(1)} %bitcast.45), channel_id=1, source_target_pairs={{0,1},{1,2},{2,3},{3,4},{4,5},{5,6},{6,7},{7,8},{8,9},{9,10},{10,1... | collective-permute-start | bytes 1572872 | tf_op jit(solution)/shard_map/ppermute | solution.py:14
  65.7 12.0 %collective-permute-start.1 = (bf16[2048,128]{1,0:T(8,128)(2,1)S(1)}, bf16[2048,128]{1,0:T(8,128)(2,1)S(1)}, u32[]{:S(2)}, u32[]{:S(2)}) collective-permute-start(bf16[2048,128]{1,0:T(8,128)(2,1)S(1)} %bitcast.46), channel_id=1, source_target_pairs={{1,0},{2,1},{3,2},{4,3},{5,4},{6,5},{7,6},{8,7},{9,8},{10,9},{11,1... | collective-permute-start | bytes 1572872 | tf_op jit(solution)/shard_map/ppermute | solution.py:15
  67.3 6.6 %copy-start.1 = (f32[4096,128]{1,0:T(8,128)}, f32[4096,128]{1,0:T(8,128)S(1)}, u32[]{:S(2)}) copy-start(f32[4096,128]{1,0:T(8,128)S(1)} %convert_dynamic-update-slice_fusion) | copy-start | bytes 6291460
  86.4 8.3 %copy-start.2 = (f32[4096,128]{1,0:T(8,128)S(1)}, f32[4096,128]{1,0:T(8,128)}, u32[]{:S(2)}) copy-start(f32[4096,128]{1,0:T(8,128)} %copy-done.1) | copy-start | bytes 6291460
where the time goes:
time: 109 us; the launch traced here: 108 us
  blocking collectives  40.1 us (37%)
  waiting for transfers between devices  27.4 us (25%)
  local copies, waits for them, and re-layouts  16.6 us (15%)
  matrix products  11.9 us (11%)
  starting transfers between devices  9.95 us (9%)
  other arithmetic  2.15 us (2%)
    all_to_all x1, blocking collectives, per_device(): lax.all_to_all(req_ids, 'dev', split_axis=2, concat_axis=0, tiled=True)  26.7 us
    all_to_all x1, waiting for transfers between devices, per_device(): lax.all_to_all(wanted_rows, 'dev', split_axis=0, concat_axis=2, tiled=True)  17 us
    psum x1, blocking collectives, per_device(): summed = lax.psum(partial_value, 'grp')  13.4 us
    gather x1, local copies, waits for them, and re-layouts, per_device(): picked = ext_blocks[tile_cols[:, 0, :]]  8.61 us
    dot_general x1, matrix products, per_device(): jnp.einsum('rtij,rtjw->riw', tiles[:, 0], picked, preferred_element_type=...  8.25 us
    ppermute x1, waiting for transfers between devices, with_halo(): before = lax.ppermute(last, axis, up)  6.56 us
    gather x1, local copies, waits for them, and re-layouts, per_device(): jnp.take(coarse_emb, lax.all_to_all(req_ids, 'dev', split_axis=2, concat_...  6.18 us
    all_to_all x1, starting transfers between devices, per_device(): lax.all_to_all(wanted_rows, 'dev', split_axis=0, concat_axis=2, tiled=True)  6.18 us
  transfers between devices with their start and end apart: 3, of which 3 were waited for; matrix products, arithmetic and copies ran while one was open for 1% of the time, Pallas kernels for 0%

commit v1 on v0

v1 whole, which is shorter than its diff:
```python
import functools

import jax
import jax.numpy as jnp
from jax import lax
from jax.experimental import pallas as pl
from jax.experimental.pallas import tpu as pltpu
from jax.sharding import PartitionSpec as P


LANES = 128
VMEM_SPEC = pl.BlockSpec(memory_space=pltpu.VMEM)
SMEM_SPEC = pl.BlockSpec(memory_space=pltpu.SMEM)
PARAMS = pltpu.CompilerParams(vmem_limit_bytes=16 * 1024 * 1024)
CHUNKS = 2


def column_of(index_ref, b):
    return jnp.transpose(jnp.broadcast_to(index_ref[b : b + 1, :], (LANES, LANES)))


def side_by_side(table_ref):
    rows = table_ref.shape[0]
    return jnp.concatenate([table_ref[: rows // 2, :], table_ref[rows // 2 :, :]], axis=1)


def rows_of(wanted, table, depth):
    lane = lax.broadcasted_iota(jnp.int16, (LANES, LANES), 1)
    one = jnp.ones((LANES, LANES), jnp.bfloat16)
    zero = jnp.zeros((LANES, LANES), jnp.bfloat16)
    low = (wanted & (depth - 1)).astype(jnp.int16)
    onehot = jnp.concatenate(
        [jnp.where(low - jnp.int16(c * LANES) == lane, one, zero) for c in range(depth // LANES)],
        axis=1,
    )
    width = table.shape[1] // 2
    found = jnp.dot(onehot, table, preferred_element_type=jnp.float32)
    return jnp.where(wanted >= depth, found[:, width:], found[:, :width])


def gather_body(asked_ref, table_ref, out_ref):
    slots = asked_ref.shape[2]
    each = LANES // slots
    table = table_ref[...]
    row = lax.broadcasted_iota(jnp.int32, (LANES, slots), 0)
    slot = lax.broadcasted_iota(jnp.int32, (LANES, slots), 1)
    chosen = lax.rem(row, slots) == slot
    for b in range(asked_ref.shape[0] // each):
        spread = jnp.concatenate(
            [jnp.broadcast_to(asked_ref[b * each + k], (slots, slots)) for k in range(each)], axis=0
        )
        wanted = jnp.sum(jnp.where(chosen, spread, 0), axis=1, keepdims=True)
        wanted = jnp.broadcast_to(wanted, (LANES, LANES))
        value = rows_of(wanted, table, table_ref.shape[0])
        out_ref[b * LANES : (b + 1) * LANES, :] = value.astype(out_ref.dtype)


def gather(asked, table):
    count = asked.size
    return pl.pallas_call(
        gather_body,
        out_shape=jax.ShapeDtypeStruct((count, table.shape[1] // 2), table.dtype),
        in_specs=[VMEM_SPEC, VMEM_SPEC],
        out_specs=VMEM_SPEC,
        compiler_params=PARAMS,
        name="gather",
    )(asked, table)


def columns_body(index_ref, *refs, first):
    out_ref = refs[-1]
    for b in range(out_ref.shape[0] // LANES):
        out_ref[b * LANES : (b + 1) * LANES, :] = column_of(index_ref, first + b)
    if len(refs) == 3:
        refs[1][...] = side_by_side(refs[0])


def columns(index, first, count, table=None):
    wide = jax.ShapeDtypeStruct((count * LANES, LANES), jnp.int32)
    shapes, arrays = (wide,), (index,)
    if table is not None:
        rows, width = table.shape
        shapes = (jax.ShapeDtypeStruct((rows // 2, 2 * width), table.dtype), wide)
        arrays = (index, table)
    return pl.pallas_call(
        functools.partial(columns_body, first=first),
        out_shape=shapes,
        in_specs=[VMEM_SPEC] * len(arrays),
        out_specs=(VMEM_SPEC,) * len(shapes),
        compiler_params=PARAMS,
        name="columns",
    )(*arrays)


def lift_body(*refs):
    table_ref, out_ref = refs[-2:]
    table = side_by_side(table_ref)
    start = 0
    for wanted_ref in refs[:-2]:
        for b in range(wanted_ref.shape[0] // LANES):
            rows = slice(b * LANES, (b + 1) * LANES)
            value = rows_of(wanted_ref[rows, :], table, table_ref.shape[0] // 2)
            out_ref[start : start + LANES, :] = value.astype(out_ref.dtype)
            start += LANES


def lift(parts, table):
    return pl.pallas_call(
        lift_body,
        out_shape=jax.ShapeDtypeStruct((sum(p.shape[0] for p in parts), table.shape[1]), table.dtype),
        in_specs=[VMEM_SPEC] * (len(parts) + 1),
        out_specs=VMEM_SPEC,
        compiler_params=PARAMS,
        name="lift",
    )(*parts, table)


def load_body(tiles_ref, out_ref, sems, *, pieces):
    each = tiles_ref.shape[0] // pieces
    copies = [
        pltpu.make_async_copy(
            tiles_ref.at[pl.ds(p * each, each)], out_ref.at[pl.ds(p * each, each)], sems.at[p]
        )
        for p in range(pieces)
    ]
    for copy in copies:
        copy.start()
    for copy in copies:
        copy.wait()


def load(tiles):
    return pl.pallas_call(
        functools.partial(load_body, pieces=4),
        out_shape=pltpu.VMEM(tiles.shape, tiles.dtype),
        in_specs=[pl.BlockSpec(memory_space=pltpu.HBM)],
        out_specs=VMEM_SPEC,
        scratch_shapes=[pltpu.SemaphoreType.DMA((4,))],
        compiler_params=pltpu.CompilerParams(vmem_limit_bytes=48 * 1024 * 1024),
        name="load",
    )(tiles)


def smooth_body(cols_ref, tiles_ref, before_ref, own_ref, after_ref, out_ref, blocks, *, base, count, unroll):
    per_row = tiles_ref.shape[1]
    half = own_ref.shape[0]
    group = lax.axis_index("grp").astype(jnp.int32)
    blocks[0:half] = before_ref[...]
    blocks[half : 2 * half] = own_ref[...]
    blocks[2 * half : 3 * half] = after_ref[...]

    def step(s, carry):
        for k in range(unroll):
            i = s * unroll + k
            r = base + i
            left = jnp.concatenate([tiles_ref[r, t] for t in range(per_row)], axis=1)
            right = jnp.concatenate([blocks[cols_ref[t, r]] for t in range(per_row)], axis=0)
            product = jnp.dot(left, right, preferred_element_type=jnp.float32)
            own = own_ref[lax.rem(r, half)].astype(jnp.float32)
            own = jnp.where(r // half == group, own, 0.0)
            out_ref[pl.ds(pl.multiple_of(i * LANES, LANES), LANES), :] = own - 0.5 * product
        return carry

    lax.fori_loop(0, count // unroll, step, 0)


def smooth(cols, tiles, before, own, after, base, count):
    half = own.shape[0]
    return pl.pallas_call(
        functools.partial(smooth_body, base=base, count=count, unroll=8),
        out_shape=jax.ShapeDtypeStruct((count * LANES, LANES), jnp.float32),
        in_specs=[SMEM_SPEC] + [VMEM_SPEC] * 4,
        out_specs=VMEM_SPEC,
        scratch_shapes=[pltpu.VMEM((3 * half, LANES, LANES), own.dtype)],
        compiler_params=PARAMS,
        name="smooth",
    )(cols, tiles, before, own, after)


def combine_body(*refs):
    out_ref = refs[-1]
    start = 0
    for mine_ref, theirs_ref in zip(refs[:-1:2], refs[1:-1:2]):
        rows = mine_ref.shape[0]
        out_ref[start : start + rows, :] = (mine_ref[...] + theirs_ref[...]).astype(out_ref.dtype)
        start += rows


def combine(pairs, dtype):
    parts = [part for pair in pairs for part in pair]
    rows = sum(mine.shape[0] for mine, _ in pairs)
    return pl.pallas_call(
        combine_body,
        out_shape=jax.ShapeDtypeStruct((rows, parts[0].shape[1]), dtype),
        in_specs=[VMEM_SPEC] * len(parts),
        out_specs=VMEM_SPEC,
        compiler_params=PARAMS,
        name="combine",
    )(*parts)


def per_device(coarse_emb, req_ids, fine_slot, tiles, tile_cols):
    devices = lax.axis_size("dev")
    slots = req_ids.shape[3]
    width = coarse_emb.shape[1]
    row_blocks = tiles.shape[0]
    index = fine_slot.reshape(-1, LANES)
    half = index.shape[0] // 2
    tiles = load(tiles[:, 0])
    asked = lax.all_to_all(
        req_ids.reshape(devices, 1, slots), "dev", split_axis=0, concat_axis=0, tiled=True
    )
    table, first = columns(index, 0, half, coarse_emb)
    wanted = gather(asked, table)
    (second,) = columns(index, half, half)
    received = lax.all_to_all(
        wanted.reshape(devices, slots, width), "dev", split_axis=0, concat_axis=0, tiled=True
    )
    lifted = lift((first, second), received.reshape(devices * slots, width))
    up = [(i, i + 1) for i in range(devices - 1)]
    down = [(i + 1, i) for i in range(devices - 1)]
    before = lax.ppermute(lifted, "dev", up).reshape(-1, LANES, width)
    after = lax.ppermute(lifted, "dev", down).reshape(-1, LANES, width)
    own = lifted.reshape(-1, LANES, width)
    cols = tile_cols[:, 0].T
    each = row_blocks // CHUNKS
    outs = []
    for c in range(CHUNKS):
        mine = smooth(cols, tiles, before, own, after, c * each, each)
        theirs = lax.ppermute(mine, "grp", [(0, 1), (1, 0)])
        outs.append((mine, theirs))
    return combine(outs, lifted.dtype)


def solution(mesh):
    return jax.shard_map(
        per_device,
        mesh=mesh,
        in_specs=(
            P("dev", None),
            P("dev", "grp", None, None),
            P("dev", "grp", None),
            P("dev", "grp", None, None, None),
            P("dev", "grp", None),
        ),
        out_specs=P("dev", None),
        check_vma=False,
    )
```

time: 109 us -> 86.8 us (0.80)
  the two profiles are of different devices: /device:TPU:1 before, /device:TPU:3 now
where the time goes in v1:
time: 86.8 us; the launch traced here: 86.4 us
  waiting for transfers between devices  37.2 us (43%)
  starting transfers between devices  33.2 us (38%)
  Pallas kernels  12.2 us (14%)
  local copies, waits for them, and re-layouts  3.76 us (4%)
    all_to_all x1, starting transfers between devices, per_device(): lax.all_to_all(req_ids.reshape(devices, 1, slots), 'dev', split_axis=0, c...  15 us
    all_to_all x1, waiting for transfers between devices, per_device(): lax.all_to_all(wanted.reshape(devices, slots, width), 'dev', split_axis=0...  14.9 us
    all_to_all x1, waiting for transfers between devices, per_device(): lax.all_to_all(req_ids.reshape(devices, 1, slots), 'dev', split_axis=0, c...  8.09 us
    ppermute x1, waiting for transfers between devices, per_device(): before = lax.ppermute(lifted, 'dev', up).reshape(-1, LANES, width)  8.05 us
    all_to_all x1, starting transfers between devices, per_device(): lax.all_to_all(wanted.reshape(devices, slots, width), 'dev', split_axis=0...  6.76 us
    ppermute x1, starting transfers between devices, per_device(): after = lax.ppermute(lifted, 'dev', down).reshape(-1, LANES, width)  4.87 us
    ppermute x2, starting transfers between devices, per_device(): theirs = lax.ppermute(mine, 'grp', [(0, 1), (1, 0)])  4.69 us
    pallas_call x2, Pallas kernels, smooth(): pl.pallas_call(functools.partial(smooth_body, base=base, count=count, unr...  4.23 us
  transfers between devices with their start and end apart: 6, of which 6 were waited for; matrix products, arithmetic and copies ran while one was open for 0% of the time, Pallas kernels for 5%

profile of v1, /device:TPU:3, one launch (start us, length us, event | category | flops | bytes accessed | tf_op | source)
XLA Modules:
  0.0 86.4 jit_solution(6097184810567714121)
XLA Ops:
  0.0 1.4 %copy.6 = s32[1,1,128,16]{3,2,1,0:T(8,128)} copy(s32[1,1,128,16]{2,3,1,0:T(8,128)} %param.6) | data formatting | bytes 16384 | tf_op args[1]
  1.4 15.0 %all-to-all-start = ((s32[128,1,16]{2,1,0:T(1,128)}), s32[128,1,16]{2,1,0:T(1,128)S(1)}, u32[]{:S(2)}, u32[]{:S(2)}) async-start(s32[128,1,16]{2,1,0:T(1,128)} %bitcast.4), calls=%async_computation | async-start | bytes 131072 | tf_op jit(solution)/shard_map/all_to_all | solution.py:210
  16.4 0.0 copy-start
  16.4 0.9 %copy-done = bf16[1024,128]{1,0:T(8,128)(2,1)S(1)} copy-done((bf16[1024,128]{1,0:T(8,128)(2,1)S(1)}, bf16[1024,128]{1,0:T(8,128)(2,1)}, u32[]{:S(2)}) %copy-start) | copy-done | bytes 262168
  17.4 0.0 copy-start.1
  17.4 0.7 copy-done.1
  18.1 0.2 columns.2
  18.3 8.1 %all-to-all-done.asked_ref = s32[128,1,16]{2,1,0:T(1,128)S(1)} async-done(((s32[128,1,16]{2,1,0:T(1,128)}), s32[128,1,16]{2,1,0:T(1,128)S(1)}, u32[]{:S(2)}, u32[]{:S(2)}) %all-to-all-start) | async-done | bytes 8224 | tf_op jit(solution)/shard_map/all_to_all | solution.py:210
  26.3 1.6 %gather.1 = bf16[2048,128]{1,0:T(8,128)(2,1)} custom-call(s32[128,1,16]{2,1,0:T(1,128)S(1)} %all-to-all-done.asked_ref, bf16[512,256]{1,0:T(8,128)(2,1)S(1)} %get-tuple-element.8.table_ref), custom_call_target="tpu_custom_call" | custom-call | tf_op jit(solution)/shard_map/gather/pallas_call | solution.py:60
  28.0 6.8 %all-to-all-start.1 = ((bf16[128,16,128]{2,1,0:T(8,128)(2,1)}), bf16[128,16,128]{2,1,0:T(8,128)(2,1)S(1)}, u32[]{:S(2)}, u32[]{:S(2)}) async-start(bf16[128,16,128]{2,1,0:T(8,128)(2,1)} %bitcast.5), calls=%async_computation.1 | async-start | bytes 1048576 | tf_op jit(solution)/shard_map/all_to_all | solution.py:216
  34.7 0.0 copy-start.2
  34.7 0.7 copy-done.2
  35.4 0.2 columns.3.refs_1_
  35.6 14.9 %all-to-all-done.1 = bf16[128,16,128]{2,1,0:T(8,128)(2,1)S(1)} async-done(((bf16[128,16,128]{2,1,0:T(8,128)(2,1)}), bf16[128,16,128]{2,1,0:T(8,128)(2,1)S(1)}, u32[]{:S(2)}, u32[]{:S(2)}) %all-to-all-start.1) | async-done | bytes 524320 | tf_op jit(solution)/shard_map/all_to_all | solution.py:216
  50.5 1.3 %lift.1 = bf16[2048,128]{1,0:T(8,128)(2,1)S(1)} custom-call(s32[1024,128]{1,0:T(8,128)S(1)} %get-tuple-element.7.refs_0_, s32[1024,128]{1,0:T(8,128)S(1)} %columns.3.refs_1_, bf16[2048,128]{1,0:T(8,128)(2,1)S(1)} %bitcast.17), custom_call_target="tpu_custom_call" | custom-call | tf_op jit(solution)/shard_map/lift/pallas_call | solution.py:108
  51.8 4.9 %collective-permute-start.1 = (bf16[2048,128]{1,0:T(8,128)(2,1)S(1)}, bf16[2048,128]{1,0:T(8,128)(2,1)S(1)}, u32[]{:S(2)}, u32[]{:S(2)}) collective-permute-start(bf16[2048,128]{1,0:T(8,128)(2,1)S(1)} %lift.1), channel_id=1, source_target_pairs={{1,0},{2,1},{3,2},{4,3},{5,4},{6,5},{7,6},{8,7},{9,8},{10,9},{11,1... | collective-permute-start | bytes 1572872 | tf_op jit(solution)/shard_map/ppermute | solution.py:223
  56.7 1.9 %collective-permute-start = (bf16[2048,128]{1,0:T(8,128)(2,1)S(1)}, bf16[2048,128]{1,0:T(8,128)(2,1)S(1)}, u32[]{:S(2)}, u32[]{:S(2)}) collective-permute-start(bf16[2048,128]{1,0:T(8,128)(2,1)S(1)} %lift.1), channel_id=1, source_target_pairs={{0,1},{1,2},{2,3},{3,4},{4,5},{5,6},{6,7},{7,8},{8,9},{9,10},{10,1... | collective-permute-start | bytes 1572872 | tf_op jit(solution)/shard_map/ppermute | solution.py:222
  58.6 0.0 copy-start.3
  58.6 3.5 %load.1.tiles_ref = bf16[32,8,128,128]{3,2,1,0:T(8,128)(2,1)S(1)} custom-call(bf16[32,8,128,128]{3,2,1,0:T(8,128)(2,1)} %bitcast.22), custom_call_target="tpu_custom_call" | custom-call | tf_op jit(solution)/shard_map/load/pallas_call | solution.py:133
  62.1 2.4 %collective-permute-done.1 = bf16[2048,128]{1,0:T(8,128)(2,1)S(1)} collective-permute-done((bf16[2048,128]{1,0:T(8,128)(2,1)S(1)}, bf16[2048,128]{1,0:T(8,128)(2,1)S(1)}, u32[]{:S(2)}, u32[]{:S(2)}) %collective-permute-start.1) | collective-permute-done | bytes 524320 | tf_op jit(solution)/shard_map/ppermute | solution.py:223
  64.6 8.1 %collective-permute-done = bf16[2048,128]{1,0:T(8,128)(2,1)S(1)} collective-permute-done((bf16[2048,128]{1,0:T(8,128)(2,1)S(1)}, bf16[2048,128]{1,0:T(8,128)(2,1)S(1)}, u32[]{:S(2)}, u32[]{:S(2)}) %collective-permute-start) | collective-permute-done | bytes 524320 | tf_op jit(solution)/shard_map/ppermute | solution.py:222
  72.6 0.0 copy-done.3
  72.6 2.1 %smooth.3.refs_2_ = f32[2048,128]{1,0:T(8,128)S(1)} custom-call(s32[8,32]{1,0:T(8,128)S(1)} %bitcast.20, bf16[32,8,128,128]{3,2,1,0:T(8,128)(2,1)S(1)} %load.1.tiles_ref, bf16[16,128,128]{2,1,0:T(8,128)(2,1)S(1)} %bitcast.15, bf16[16,128,128]{2,1,0:T(8,128)(2,1)S(1)} %bitcast.11, bf16[16,128,128]{2,1,0:T(8,128)(2,1)S(1)} %bitcast.13), custom_call_target="tpu_custom_call" | custom-call | tf_op jit(solution)/shard_map/smooth/pallas_call | solution.py:169
  74.7 2.1 %smooth.2.refs_0_ = f32[2048,128]{1,0:T(8,128)S(1)} custom-call(s32[8,32]{1,0:T(8,128)S(1)} %bitcast.21, bf16[32,8,128,128]{3,2,1,0:T(8,128)(2,1)S(1)} %load.1.tiles_ref, bf16[16,128,128]{2,1,0:T(8,128)(2,1)S(1)} %bitcast.16, bf16[16,128,128]{2,1,0:T(8,128)(2,1)S(1)} %bitcast.12, bf16[16,128,128]{2,1,0:T(8,128)(2,1)S(1)} %bitcast.14), custom_call_target="tpu_custom_call" | custom-call | tf_op jit(solution)/shard_map/smooth/pallas_call | solution.py:169
  76.9 4.6 %collective-permute-start.2 = (f32[2048,128]{1,0:T(8,128)S(1)}, f32[2048,128]{1,0:T(8,128)S(1)}, u32[]{:S(2)}, u32[]{:S(2)}) collective-permute-start(f32[2048,128]{1,0:T(8,128)S(1)} %smooth.2.refs_0_), channel_id=1, source_target_pairs={{0,128},{128,0},{1,129},{129,1},{2,130},{130,2},{3,131},{131,3},{4... | collective-permute-start | bytes 3145736 | tf_op jit(solution)/shard_map/ppermute | solution.py:230
  81.5 0.1 collective-permute-start.3
  81.6 2.2 %collective-permute-done.2.refs_1_ = f32[2048,128]{1,0:T(8,128)S(1)} collective-permute-done((f32[2048,128]{1,0:T(8,128)S(1)}, f32[2048,128]{1,0:T(8,128)S(1)}, u32[]{:S(2)}, u32[]{:S(2)}) %collective-permute-start.2) | collective-permute-done | bytes 1048608 | tf_op jit(solution)/shard_map/ppermute | solution.py:230
  83.7 1.5 %collective-permute-done.3.refs_3_ = f32[2048,128]{1,0:T(8,128)S(1)} collective-permute-done((f32[2048,128]{1,0:T(8,128)S(1)}, f32[2048,128]{1,0:T(8,128)S(1)}, u32[]{:S(2)}, u32[]{:S(2)}) %collective-permute-start.3) | collective-permute-done | bytes 1048608 | tf_op jit(solution)/shard_map/ppermute | solution.py:230
  85.2 1.2 %combine.1 = bf16[4096,128]{1,0:T(8,128)(2,1)} custom-call(f32[2048,128]{1,0:T(8,128)S(1)} %smooth.2.refs_0_, f32[2048,128]{1,0:T(8,128)S(1)} %collective-permute-done.2.refs_1_, f32[2048,128]{1,0:T(8,128)S(1)} %smooth.3.refs_2_, f32[2048,128]{1,0:T(8,128)S(1)} %collective-permute-done.3.refs_3_), custom_call_target="tpu_custom_call" | custom-call | tf_op jit(solution)/shard_map/combine/pallas_call | solution.py:192
Async XLA Ops:
  1.4 24.9 %all-to-all-start = ((s32[128,1,16]{2,1,0:T(1,128)}), s32[128,1,16]{2,1,0:T(1,128)S(1)}, u32[]{:S(2)}, u32[]{:S(2)}) async-start(s32[128,1,16]{2,1,0:T(1,128)} %bitcast.4), calls=%async_computation | async-start | bytes 131072 | tf_op jit(solution)/shard_map/all_to_all | solution.py:210
  16.4 1.0 %copy-start = (bf16[1024,128]{1,0:T(8,128)(2,1)S(1)}, bf16[1024,128]{1,0:T(8,128)(2,1)}, u32[]{:S(2)}) copy-start(bf16[1024,128]{1,0:T(8,128)(2,1)} %refs_0_.1) | copy-start | bytes 786436
  17.4 0.7 copy-start.1
  28.0 22.6 %all-to-all-start.1 = ((bf16[128,16,128]{2,1,0:T(8,128)(2,1)}), bf16[128,16,128]{2,1,0:T(8,128)(2,1)S(1)}, u32[]{:S(2)}, u32[]{:S(2)}) async-start(bf16[128,16,128]{2,1,0:T(8,128)(2,1)} %bitcast.5), calls=%async_computation.1 | async-start | bytes 1048576 | tf_op jit(solution)/shard_map/all_to_all | solution.py:216
  34.7 0.7 copy-start.2
  51.8 12.8 %collective-permute-start.1 = (bf16[2048,128]{1,0:T(8,128)(2,1)S(1)}, bf16[2048,128]{1,0:T(8,128)(2,1)S(1)}, u32[]{:S(2)}, u32[]{:S(2)}) collective-permute-start(bf16[2048,128]{1,0:T(8,128)(2,1)S(1)} %lift.1), channel_id=1, source_target_pairs={{1,0},{2,1},{3,2},{4,3},{5,4},{6,5},{7,6},{8,7},{9,8},{10,9},{11,1... | collective-permute-start | bytes 1572872 | tf_op jit(solution)/shard_map/ppermute | solution.py:223
  56.7 16.0 %collective-permute-start = (bf16[2048,128]{1,0:T(8,128)(2,1)S(1)}, bf16[2048,128]{1,0:T(8,128)(2,1)S(1)}, u32[]{:S(2)}, u32[]{:S(2)}) collective-permute-start(bf16[2048,128]{1,0:T(8,128)(2,1)S(1)} %lift.1), channel_id=1, source_target_pairs={{0,1},{1,2},{2,3},{3,4},{4,5},{5,6},{6,7},{7,8},{8,9},{9,10},{10,1... | collective-permute-start | bytes 1572872 | tf_op jit(solution)/shard_map/ppermute | solution.py:222
  58.6 14.0 %copy-start.3 = (s32[32,1,8]{0,2,1:T(8,128)S(1)}, s32[32,1,8]{0,2,1:T(8,128)}, u32[]{:S(2)}) copy-start(s32[32,1,8]{0,2,1:T(8,128)} %param.9) | copy-start | bytes 3076
  76.9 6.9 %collective-permute-start.2 = (f32[2048,128]{1,0:T(8,128)S(1)}, f32[2048,128]{1,0:T(8,128)S(1)}, u32[]{:S(2)}, u32[]{:S(2)}) collective-permute-start(f32[2048,128]{1,0:T(8,128)S(1)} %smooth.2.refs_0_), channel_id=1, source_target_pairs={{0,128},{128,0},{1,129},{129,1},{2,130},{130,2},{3,131},{131,3},{4... | collective-permute-start | bytes 3145736 | tf_op jit(solution)/shard_map/ppermute | solution.py:230
  81.5 3.8 %collective-permute-start.3 = (f32[2048,128]{1,0:T(8,128)S(1)}, f32[2048,128]{1,0:T(8,128)S(1)}, u32[]{:S(2)}, u32[]{:S(2)}) collective-permute-start(f32[2048,128]{1,0:T(8,128)S(1)} %smooth.3.refs_2_), channel_id=1, source_target_pairs={{0,128},{128,0},{1,129},{129,1},{2,130},{130,2},{3,131},{131,3},{4... | collective-permute-start | bytes 3145736 | tf_op jit(solution)/shard_map/ppermute | solution.py:230

commit v2 on v1

--- a/solution.py
+++ b/solution.py
@@ -12,7 +12,8 @@
 VMEM_SPEC = pl.BlockSpec(memory_space=pltpu.VMEM)
 SMEM_SPEC = pl.BlockSpec(memory_space=pltpu.SMEM)
 PARAMS = pltpu.CompilerParams(vmem_limit_bytes=16 * 1024 * 1024)
-CHUNKS = 2
+CHUNKS = (8, 8, 8, 8)
+UNROLL = 8
 
 
 def column_of(index_ref, b):
@@ -141,62 +142,97 @@
     )(tiles)
 
 
-def smooth_body(cols_ref, tiles_ref, before_ref, own_ref, after_ref, out_ref, blocks, *, base, count, unroll):
+def product_rows(cols_ref, tiles_ref, blocks_ref, out_ref, base):
     per_row = tiles_ref.shape[1]
-    half = own_ref.shape[0]
+    half = blocks_ref.shape[0] // 3
+    count = out_ref.shape[0] // LANES
     group = lax.axis_index("grp").astype(jnp.int32)
-    blocks[0:half] = before_ref[...]
-    blocks[half : 2 * half] = own_ref[...]
-    blocks[2 * half : 3 * half] = after_ref[...]
 
     def step(s, carry):
-        for k in range(unroll):
-            i = s * unroll + k
+        for k in range(UNROLL):
+            i = s * UNROLL + k
             r = base + i
             left = jnp.concatenate([tiles_ref[r, t] for t in range(per_row)], axis=1)
-            right = jnp.concatenate([blocks[cols_ref[t, r]] for t in range(per_row)], axis=0)
+            right = jnp.concatenate([blocks_ref[cols_ref[t, r]] for t in range(per_row)], axis=0)
             product = jnp.dot(left, right, preferred_element_type=jnp.float32)
-            own = own_ref[lax.rem(r, half)].astype(jnp.float32)
+            own = blocks_ref[half + lax.rem(r, half)].astype(jnp.float32)
             own = jnp.where(r // half == group, own, 0.0)
             out_ref[pl.ds(pl.multiple_of(i * LANES, LANES), LANES), :] = own - 0.5 * product
         return carry
 
-    lax.fori_loop(0, count // unroll, step, 0)
-
-
-def smooth(cols, tiles, before, own, after, base, count):
+    lax.fori_loop(0, count // UNROLL, step, 0)
+
+
+def first_body(cols_ref, tiles_ref, before_ref, own_ref, after_ref, out_ref, blocks_ref):
+    half = own_ref.shape[0]
+    place = lax.axis_index("dev")
+    zeros = jnp.zeros(own_ref.shape, own_ref.dtype)
+    blocks_ref[0:half] = jnp.where(place > 0, before_ref[...], zeros)
+    blocks_ref[half : 2 * half] = own_ref[...]
+    blocks_ref[2 * half : 3 * half] = jnp.where(
+        place < lax.axis_size("dev") - 1, after_ref[...], zeros
+    )
+    product_rows(cols_ref, tiles_ref, blocks_ref, out_ref, 0)
+
+
+def first_rows(cols, tiles, before, own, after, count):
     half = own.shape[0]
     return pl.pallas_call(
-        functools.partial(smooth_body, base=base, count=count, unroll=8),
+        first_body,
+        out_shape=(
+            jax.ShapeDtypeStruct((count * LANES, LANES), jnp.float32),
+            jax.ShapeDtypeStruct((3 * half, LANES, LANES), own.dtype),
+        ),
+        in_specs=[SMEM_SPEC] + [VMEM_SPEC] * 4,
+        out_specs=(VMEM_SPEC, VMEM_SPEC),
+        compiler_params=PARAMS,
+        name="first_rows",
+    )(cols, tiles, before, own, after)
+
+
+def more_body(cols_ref, tiles_ref, blocks_ref, out_ref, *, base):
+    product_rows(cols_ref, tiles_ref, blocks_ref, out_ref, base)
+
+
+def more_rows(cols, tiles, blocks, base, count):
+    return pl.pallas_call(
+        functools.partial(more_body, base=base),
         out_shape=jax.ShapeDtypeStruct((count * LANES, LANES), jnp.float32),
-        in_specs=[SMEM_SPEC] + [VMEM_SPEC] * 4,
-        out_specs=VMEM_SPEC,
-        scratch_shapes=[pltpu.VMEM((3 * half, LANES, LANES), own.dtype)],
-        compiler_params=PARAMS,
-        name="smooth",
-    )(cols, tiles, before, own, after)
-
-
-def combine_body(*refs):
-    out_ref = refs[-1]
+        in_specs=[SMEM_SPEC] + [VMEM_SPEC] * 2,
+        out_specs=VMEM_SPEC,
+        compiler_params=PARAMS,
+        name="more_rows",
+    )(cols, tiles, blocks)
+
+
+def combine_body(*refs, first):
+    out_ref, buffer, sem = refs[-3:]
+    pairs = (len(refs) - 3) // 2
     start = 0
-    for mine_ref, theirs_ref in zip(refs[:-1:2], refs[1:-1:2]):
+    for mine_ref, theirs_ref in zip(refs[: 2 * pairs : 2], refs[1 : 2 * pairs : 2]):
         rows = mine_ref.shape[0]
-        out_ref[start : start + rows, :] = (mine_ref[...] + theirs_ref[...]).astype(out_ref.dtype)
+        buffer[start : start + rows, :] = (mine_ref[...] + theirs_ref[...]).astype(buffer.dtype)
         start += rows
-
-
-def combine(pairs, dtype):
+    copy = pltpu.make_async_copy(buffer, out_ref.at[pl.ds(first, start)], sem)
+    copy.start()
+    copy.wait()
+
+
+def combine(pairs, out, rows, first, dtype):
     parts = [part for pair in pairs for part in pair]
-    rows = sum(mine.shape[0] for mine, _ in pairs)
-    return pl.pallas_call(
-        combine_body,
-        out_shape=jax.ShapeDtypeStruct((rows, parts[0].shape[1]), dtype),
-        in_specs=[VMEM_SPEC] * len(parts),
-        out_specs=VMEM_SPEC,
+    count, width = sum(mine.shape[0] for mine, _ in pairs), parts[0].shape[1]
+    anywhere = pl.BlockSpec(memory_space=pltpu.HBM)
+    before = [] if out is None else [out]
+    return pl.pallas_call(
+        functools.partial(combine_body, first=first),
+        out_shape=jax.ShapeDtypeStruct((rows, width), dtype),
+        in_specs=[VMEM_SPEC] * len(parts) + [anywhere] * len(before),
+        out_specs=anywhere,
+        input_output_aliases={len(parts): 0} if before else {},
+        scratch_shapes=[pltpu.VMEM((count, width), dtype), pltpu.SemaphoreType.DMA],
         compiler_params=PARAMS,
         name="combine",
-    )(*parts)
+    )(*parts, *before)
 
 
 def per_device(coarse_emb, req_ids, fine_slot, tiles, tile_cols):
@@ -218,18 +254,23 @@
     )
     lifted = lift((first, second), received.reshape(devices * slots, width))
     up = [(i, i + 1) for i in range(devices - 1)]
-    down = [(i + 1, i) for i in range(devices - 1)]
+    down = [((i + 1) % devices, i) for i in range(devices)]
     before = lax.ppermute(lifted, "dev", up).reshape(-1, LANES, width)
     after = lax.ppermute(lifted, "dev", down).reshape(-1, LANES, width)
     own = lifted.reshape(-1, LANES, width)
     cols = tile_cols[:, 0].T
-    each = row_blocks // CHUNKS
-    outs = []
-    for c in range(CHUNKS):
-        mine = smooth(cols, tiles, before, own, after, c * each, each)
-        theirs = lax.ppermute(mine, "grp", [(0, 1), (1, 0)])
-        outs.append((mine, theirs))
-    return combine(outs, lifted.dtype)
+    parts = []
+    base = 0
+    for c, count in enumerate(CHUNKS):
+        if c == 0:
+            mine, blocks = first_rows(cols, tiles, before, own, after, count)
+        else:
+            mine = more_rows(cols, tiles, blocks, base, count)
+        parts.append((mine, lax.ppermute(mine, "grp", [(0, 1), (1, 0)])))
+        base += count
+    rows = row_blocks * LANES
+    out = combine(parts[:-1], None, rows, 0, lifted.dtype)
+    return combine(parts[-1:], out, rows, rows - parts[-1][0].shape[0], lifted.dtype)
 
 
 def solution(mesh):

time: 86.8 us -> 84.8 us (0.977)
  waiting for transfers between devices: 37.2 us -> 34.5 us
  Pallas kernels: 12.2 us -> 14 us
  starting transfers between devices: 33.2 us -> 32 us
    ppermute x2 -> x4, waiting for transfers between devices: 3.69 us -> 1.02 us  [per_device(): parts.append((mine, lax.ppermute(mine, 'grp', [(0, 1), (1, 0)])))]
    pallas_call x3 -> x6, Pallas kernels: 5.38 us -> 7.27 us  [the longest x3 3.93 us: more_rows(): pl.pallas_call(functools.partial(more_body, base=base), out_shape=jax.Sha...]
    ppermute x1, starting transfers between devices: 4.87 us -> 3.04 us  [per_device(): after = lax.ppermute(lifted, 'dev', down).reshape(-1, LANES, width)]
    ppermute x2 -> x4, starting transfers between devices: 4.69 us -> 5.28 us  [per_device(): parts.append((mine, lax.ppermute(mine, 'grp', [(0, 1), (1, 0)])))]
  transfers between devices with their start and end apart: 6 -> 8, of which waited for: 6 -> 6; matrix products, arithmetic and copies ran while one was open for 0% -> 0% of each run, Pallas kernels for 5% -> 7%
where the time goes in v2:
time: 84.8 us; the launch traced here: 84.4 us
  waiting for transfers between devices  34.5 us (41%)
  starting transfers between devices  32 us (38%)
  Pallas kernels  14 us (17%)
  local copies, waits for them, and re-layouts  3.76 us (4%)
    all_to_all x1, starting transfers between devices, per_device(): lax.all_to_all(req_ids.reshape(devices, 1, slots), 'dev', split_axis=0, c...  15 us
    all_to_all x1, waiting for transfers between devices, per_device(): lax.all_to_all(wanted.reshape(devices, slots, width), 'dev', split_axis=0...  14.9 us
    all_to_all x1, waiting for transfers between devices, per_device(): lax.all_to_all(req_ids.reshape(devices, 1, slots), 'dev', split_axis=0, c...  8.09 us
    ppermute x1, waiting for transfers between devices, per_device(): before = lax.ppermute(lifted, 'dev', up).reshape(-1, LANES, width)  8.02 us
    all_to_all x1, starting transfers between devices, per_device(): lax.all_to_all(wanted.reshape(devices, slots, width), 'dev', split_axis=0...  6.76 us
    ppermute x4, starting transfers between devices, per_device(): parts.append((mine, lax.ppermute(mine, 'grp', [(0, 1), (1, 0)])))  5.28 us
    pallas_call x3, Pallas kernels, more_rows(): pl.pallas_call(functools.partial(more_body, base=base), out_shape=jax.Sha...  3.93 us
    unnamed x9, local copies, waits for them, and re-layouts  3.76 us
  transfers between devices with their start and end apart: 8, of which 6 were waited for; matrix products, arithmetic and copies ran while one was open for 0% of the time, Pallas kernels for 7%

profile of v2, /device:TPU:3, one launch (start us, length us, event | category | flops | bytes accessed | tf_op | source)
XLA Modules:
  0.0 84.4 jit_solution(3638073234049960408)
XLA Ops:
  0.0 1.4 %copy.7 = s32[1,1,128,16]{3,2,1,0:T(8,128)} copy(s32[1,1,128,16]{2,3,1,0:T(8,128)} %param.6) | data formatting | bytes 16384 | tf_op args[1]
  1.4 15.0 %all-to-all-start = ((s32[128,1,16]{2,1,0:T(1,128)}), s32[128,1,16]{2,1,0:T(1,128)S(1)}, u32[]{:S(2)}, u32[]{:S(2)}) async-start(s32[128,1,16]{2,1,0:T(1,128)} %bitcast.5), calls=%async_computation | async-start | bytes 131072 | tf_op jit(solution)/shard_map/all_to_all | solution.py:246
  16.4 0.0 copy-start
  16.4 0.9 %copy-done = bf16[1024,128]{1,0:T(8,128)(2,1)S(1)} copy-done((bf16[1024,128]{1,0:T(8,128)(2,1)S(1)}, bf16[1024,128]{1,0:T(8,128)(2,1)}, u32[]{:S(2)}) %copy-start) | copy-done | bytes 262168
  17.4 0.7 copy-done.2
  18.1 0.2 columns.2
  18.3 8.1 %all-to-all-done.asked_ref = s32[128,1,16]{2,1,0:T(1,128)S(1)} async-done(((s32[128,1,16]{2,1,0:T(1,128)}), s32[128,1,16]{2,1,0:T(1,128)S(1)}, u32[]{:S(2)}, u32[]{:S(2)}) %all-to-all-start) | async-done | bytes 8224 | tf_op jit(solution)/shard_map/all_to_all | solution.py:246
  26.3 1.6 %gather.1 = bf16[2048,128]{1,0:T(8,128)(2,1)} custom-call(s32[128,1,16]{2,1,0:T(1,128)S(1)} %all-to-all-done.asked_ref, bf16[512,256]{1,0:T(8,128)(2,1)S(1)} %get-tuple-element.10.table_ref), custom_call_target="tpu_custom_call" | custom-call | tf_op jit(solution)/shard_map/gather/pallas_call | solution.py:61
  28.0 6.8 %all-to-all-start.1 = ((bf16[128,16,128]{2,1,0:T(8,128)(2,1)}), bf16[128,16,128]{2,1,0:T(8,128)(2,1)S(1)}, u32[]{:S(2)}, u32[]{:S(2)}) async-start(bf16[128,16,128]{2,1,0:T(8,128)(2,1)} %bitcast.6), calls=%async_computation.1 | async-start | bytes 1048576 | tf_op jit(solution)/shard_map/all_to_all | solution.py:252
  34.7 0.0 copy-start.3
  34.7 0.7 copy-done.3
  35.4 0.2 columns.3.refs_1_
  35.6 14.9 %all-to-all-done.1 = bf16[128,16,128]{2,1,0:T(8,128)(2,1)S(1)} async-done(((bf16[128,16,128]{2,1,0:T(8,128)(2,1)}), bf16[128,16,128]{2,1,0:T(8,128)(2,1)S(1)}, u32[]{:S(2)}, u32[]{:S(2)}) %all-to-all-start.1) | async-done | bytes 524320 | tf_op jit(solution)/shard_map/all_to_all | solution.py:252
  50.5 1.3 %lift.1 = bf16[2048,128]{1,0:T(8,128)(2,1)S(1)} custom-call(s32[1024,128]{1,0:T(8,128)S(1)} %get-tuple-element.9.refs_0_, s32[1024,128]{1,0:T(8,128)S(1)} %columns.3.refs_1_, bf16[2048,128]{1,0:T(8,128)(2,1)S(1)} %bitcast.12), custom_call_target="tpu_custom_call" | custom-call | tf_op jit(solution)/shard_map/lift/pallas_call | solution.py:109
  51.8 3.0 %collective-permute-start.1 = (bf16[2048,128]{1,0:T(8,128)(2,1)S(1)}, bf16[2048,128]{1,0:T(8,128)(2,1)S(1)}, u32[]{:S(2)}, u32[]{:S(2)}) collective-permute-start(bf16[2048,128]{1,0:T(8,128)(2,1)S(1)} %lift.1), channel_id=1, source_target_pairs={{1,0},{2,1},{3,2},{4,3},{5,4},{6,5},{7,6},{8,7},{9,8},{10,9},{11,1... | collective-permute-start | bytes 1572872 | tf_op jit(solution)/shard_map/ppermute | solution.py:259
  54.8 1.9 %collective-permute-start = (bf16[2048,128]{1,0:T(8,128)(2,1)S(1)}, bf16[2048,128]{1,0:T(8,128)(2,1)S(1)}, u32[]{:S(2)}, u32[]{:S(2)}) collective-permute-start(bf16[2048,128]{1,0:T(8,128)(2,1)S(1)} %lift.1), channel_id=1, source_target_pairs={{0,1},{1,2},{2,3},{3,4},{4,5},{5,6},{6,7},{7,8},{8,9},{9,10},{10,1... | collective-permute-start | bytes 1572872 | tf_op jit(solution)/shard_map/ppermute | solution.py:258
  56.7 0.0 copy-start.1
  56.8 3.5 %load.1.tiles_ref = bf16[32,8,128,128]{3,2,1,0:T(8,128)(2,1)S(1)} custom-call(bf16[32,8,128,128]{3,2,1,0:T(8,128)(2,1)} %bitcast.21), custom_call_target="tpu_custom_call" | custom-call | tf_op jit(solution)/shard_map/load/pallas_call | solution.py:134
  60.3 2.5 %collective-permute-done.1 = bf16[2048,128]{1,0:T(8,128)(2,1)S(1)} collective-permute-done((bf16[2048,128]{1,0:T(8,128)(2,1)S(1)}, bf16[2048,128]{1,0:T(8,128)(2,1)S(1)}, u32[]{:S(2)}, u32[]{:S(2)}) %collective-permute-start.1) | collective-permute-done | bytes 524320 | tf_op jit(solution)/shard_map/ppermute | solution.py:259
  62.7 8.0 %collective-permute-done = bf16[2048,128]{1,0:T(8,128)(2,1)S(1)} collective-permute-done((bf16[2048,128]{1,0:T(8,128)(2,1)S(1)}, bf16[2048,128]{1,0:T(8,128)(2,1)S(1)}, u32[]{:S(2)}, u32[]{:S(2)}) %collective-permute-start) | collective-permute-done | bytes 524320 | tf_op jit(solution)/shard_map/ppermute | solution.py:258
  70.8 1.6 %first_rows.1 = (f32[1024,128]{1,0:T(8,128)S(1)}, bf16[48,128,128]{2,1,0:T(8,128)(2,1)S(1)}) custom-call(s32[8,32]{1,0:T(8,128)S(1)} %bitcast.15, bf16[32,8,128,128]{3,2,1,0:T(8,128)(2,1)S(1)} %load.1.tiles_ref, bf16[16,128,128]{2,1,0:T(8,128)(2,1)S(1)} %bitcast.14, bf16[16,128,128]{2,1,0:T(8,128)(2,1)S(1)} %bitcast.11, bf16[16,128,128]{2,1,0:T(8,128)(2,1)S(1)} %bitcast.13), custom_call_target="tpu_custom_call" | custom-call | tf_op jit(solution)/shard_map/first_rows/pallas_call | solution.py:180
  72.3 1.3 %more_rows.5.refs_4_ = f32[1024,128]{1,0:T(8,128)S(1)} custom-call(s32[8,32]{1,0:T(8,128)S(1)} %bitcast.16, bf16[32,8,128,128]{3,2,1,0:T(8,128)(2,1)S(1)} %load.1.tiles_ref, bf16[48,128,128]{2,1,0:T(8,128)(2,1)S(1)} %get-tuple-element.11.blocks_ref), custom_call_target="tpu_custom_call" | custom-call | tf_op jit(solution)/shard_map/more_rows/pallas_call | solution.py:198
  73.6 1.3 %more_rows.4.refs_2_ = f32[1024,128]{1,0:T(8,128)S(1)} custom-call(s32[8,32]{1,0:T(8,128)S(1)} %bitcast.17, bf16[32,8,128,128]{3,2,1,0:T(8,128)(2,1)S(1)} %load.1.tiles_ref, bf16[48,128,128]{2,1,0:T(8,128)(2,1)S(1)} %get-tuple-element.11.blocks_ref), custom_call_target="tpu_custom_call" | custom-call | tf_op jit(solution)/shard_map/more_rows/pallas_call | solution.py:198
  75.0 4.6 %collective-permute-start.4 = (f32[1024,128]{1,0:T(8,128)S(1)}, f32[1024,128]{1,0:T(8,128)S(1)}, u32[]{:S(2)}, u32[]{:S(2)}) collective-permute-start(f32[1024,128]{1,0:T(8,128)S(1)} %more_rows.4.refs_2_), channel_id=1, source_target_pairs={{0,128},{128,0},{1,129},{129,1},{2,130},{130,2},{3,131},{131,3},{4... | collective-permute-start | bytes 1572872 | tf_op jit(solution)/shard_map/ppermute | solution.py:269
  79.5 0.1 collective-permute-start.5
  79.6 0.4 collective-permute-start.3
  80.1 1.3 %more_rows.3.refs_0_ = f32[1024,128]{1,0:T(8,128)S(1)} custom-call(s32[8,32]{1,0:T(8,128)S(1)} %bitcast.18, bf16[32,8,128,128]{3,2,1,0:T(8,128)(2,1)S(1)} %load.1.tiles_ref, bf16[48,128,128]{2,1,0:T(8,128)(2,1)S(1)} %get-tuple-element.11.blocks_ref), custom_call_target="tpu_custom_call" | custom-call | tf_op jit(solution)/shard_map/more_rows/pallas_call | solution.py:198
  81.4 0.2 collective-permute-start.2
  81.6 0.3 collective-permute-done.5.refs_5_
  81.8 0.7 collective-permute-done.3.refs_1_
  82.6 1.0 %combine.2.refs_2_ = bf16[4096,128]{1,0:T(8,128)(2,1)} custom-call(f32[1024,128]{1,0:T(8,128)S(1)} %get-tuple-element.12.refs_0_, f32[1024,128]{1,0:T(8,128)S(1)} %collective-permute-done.3.refs_1_, f32[1024,128]{1,0:T(8,128)S(1)} %more_rows.4.refs_2_, f32[1024,128]{1,0:T(8,128)S(1)} %collective-permute-done.4.refs_3_, f32[1024,128]{1,0:T(8,128)S(1)} %more_rows.5.refs_4_, ...), custom_call_target="tpu_custom_call" | custom-call | tf_op jit(solution)/shard_map/combine/pallas_call | solution.py:226
  83.6 0.8 combine.3
  (4 shorter events, 0.0 us)
Async XLA Ops:
  1.4 24.9 %all-to-all-start = ((s32[128,1,16]{2,1,0:T(1,128)}), s32[128,1,16]{2,1,0:T(1,128)S(1)}, u32[]{:S(2)}, u32[]{:S(2)}) async-start(s32[128,1,16]{2,1,0:T(1,128)} %bitcast.5), calls=%async_computation | async-start | bytes 131072 | tf_op jit(solution)/shard_map/all_to_all | solution.py:246
  16.4 1.0 %copy-start = (bf16[1024,128]{1,0:T(8,128)(2,1)S(1)}, bf16[1024,128]{1,0:T(8,128)(2,1)}, u32[]{:S(2)}) copy-start(bf16[1024,128]{1,0:T(8,128)(2,1)} %refs_0_.1) | copy-start | bytes 786436
  17.4 0.7 copy-start.2
  28.0 22.6 %all-to-all-start.1 = ((bf16[128,16,128]{2,1,0:T(8,128)(2,1)}), bf16[128,16,128]{2,1,0:T(8,128)(2,1)S(1)}, u32[]{:S(2)}, u32[]{:S(2)}) async-start(bf16[128,16,128]{2,1,0:T(8,128)(2,1)} %bitcast.6), calls=%async_computation.1 | async-start | bytes 1048576 | tf_op jit(solution)/shard_map/all_to_all | solution.py:252
  34.7 0.7 copy-start.3
  51.8 11.0 %collective-permute-start.1 = (bf16[2048,128]{1,0:T(8,128)(2,1)S(1)}, bf16[2048,128]{1,0:T(8,128)(2,1)S(1)}, u32[]{:S(2)}, u32[]{:S(2)}) collective-permute-start(bf16[2048,128]{1,0:T(8,128)(2,1)S(1)} %lift.1), channel_id=1, source_target_pairs={{1,0},{2,1},{3,2},{4,3},{5,4},{6,5},{7,6},{8,7},{9,8},{10,9},{11,1... | collective-permute-start | bytes 1572872 | tf_op jit(solution)/shard_map/ppermute | solution.py:259
  54.8 15.9 %collective-permute-start = (bf16[2048,128]{1,0:T(8,128)(2,1)S(1)}, bf16[2048,128]{1,0:T(8,128)(2,1)S(1)}, u32[]{:S(2)}, u32[]{:S(2)}) collective-permute-start(bf16[2048,128]{1,0:T(8,128)(2,1)S(1)} %lift.1), channel_id=1, source_target_pairs={{0,1},{1,2},{2,3},{3,4},{4,5},{5,6},{6,7},{7,8},{8,9},{9,10},{10,1... | collective-permute-start | bytes 1572872 | tf_op jit(solution)/shard_map/ppermute | solution.py:258
  56.7 14.0 %copy-start.1 = (s32[32,1,8]{0,2,1:T(8,128)S(1)}, s32[32,1,8]{0,2,1:T(8,128)}, u32[]{:S(2)}) copy-start(s32[32,1,8]{0,2,1:T(8,128)} %param.9) | copy-start | bytes 3076
  75.0 6.6 %collective-permute-start.4 = (f32[1024,128]{1,0:T(8,128)S(1)}, f32[1024,128]{1,0:T(8,128)S(1)}, u32[]{:S(2)}, u32[]{:S(2)}) collective-permute-start(f32[1024,128]{1,0:T(8,128)S(1)} %more_rows.4.refs_2_), channel_id=1, source_target_pairs={{0,128},{128,0},{1,129},{129,1},{2,130},{130,2},{3,131},{131,3},{4... | collective-permute-start | bytes 1572872 | tf_op jit(solution)/shard_map/ppermute | solution.py:269
  79.5 2.3 %collective-permute-start.5 = (f32[1024,128]{1,0:T(8,128)S(1)}, f32[1024,128]{1,0:T(8,128)S(1)}, u32[]{:S(2)}, u32[]{:S(2)}) collective-permute-start(f32[1024,128]{1,0:T(8,128)S(1)} %more_rows.5.refs_4_), channel_id=1, source_target_pairs={{0,128},{128,0},{1,129},{129,1},{2,130},{130,2},{3,131},{131,3},{4... | collective-permute-start | bytes 1572872 | tf_op jit(solution)/shard_map/ppermute | solution.py:269
  79.6 2.9 %collective-permute-start.3 = (f32[1024,128]{1,0:T(8,128)S(1)}, f32[1024,128]{1,0:T(8,128)S(1)}, u32[]{:S(2)}, u32[]{:S(2)}) collective-permute-start(f32[1024,128]{1,0:T(8,128)S(1)} %get-tuple-element.12.refs_0_), channel_id=1, source_target_pairs={{0,128},{128,0},{1,129},{129,1},{2,130},{130,2},{3,131},{131,3},{4... | collective-permute-start | bytes 1572872 | tf_op jit(solution)/shard_map/ppermute | solution.py:269
  81.4 2.2 %collective-permute-start.2 = (f32[1024,128]{1,0:T(8,128)S(1)}, f32[1024,128]{1,0:T(8,128)S(1)}, u32[]{:S(2)}, u32[]{:S(2)}) collective-permute-start(f32[1024,128]{1,0:T(8,128)S(1)} %more_rows.3.refs_0_), channel_id=1, source_target_pairs={{0,128},{128,0},{1,129},{129,1},{2,130},{130,2},{3,131},{131,3},{4... | collective-permute-start | bytes 1572872 | tf_op jit(solution)/shard_map/ppermute | solution.py:269

commit v3 on v2

--- a/solution.py
+++ b/solution.py
@@ -12,8 +12,7 @@
 VMEM_SPEC = pl.BlockSpec(memory_space=pltpu.VMEM)
 SMEM_SPEC = pl.BlockSpec(memory_space=pltpu.SMEM)
 PARAMS = pltpu.CompilerParams(vmem_limit_bytes=16 * 1024 * 1024)
-CHUNKS = (8, 8, 8, 8)
-UNROLL = 8
+CHUNKS = (8, 12, 12)
 
 
 def column_of(index_ref, b):
@@ -148,34 +147,29 @@
     count = out_ref.shape[0] // LANES
     group = lax.axis_index("grp").astype(jnp.int32)
 
-    def step(s, carry):
-        for k in range(UNROLL):
-            i = s * UNROLL + k
-            r = base + i
-            left = jnp.concatenate([tiles_ref[r, t] for t in range(per_row)], axis=1)
-            right = jnp.concatenate([blocks_ref[cols_ref[t, r]] for t in range(per_row)], axis=0)
-            product = jnp.dot(left, right, preferred_element_type=jnp.float32)
-            own = blocks_ref[half + lax.rem(r, half)].astype(jnp.float32)
-            own = jnp.where(r // half == group, own, 0.0)
-            out_ref[pl.ds(pl.multiple_of(i * LANES, LANES), LANES), :] = own - 0.5 * product
-        return carry
-
-    lax.fori_loop(0, count // UNROLL, step, 0)
-
-
-def first_body(cols_ref, tiles_ref, before_ref, own_ref, after_ref, out_ref, blocks_ref):
+    for i in range(count):
+        r = base + i
+        left = jnp.concatenate([tiles_ref[r, t] for t in range(per_row)], axis=1)
+        right = jnp.concatenate([blocks_ref[cols_ref[t, r]] for t in range(per_row)], axis=0)
+        product = jnp.dot(left, right, preferred_element_type=jnp.float32)
+        own = blocks_ref[half + r % half].astype(jnp.float32)
+        own = jnp.where(group == r // half, own, 0.0)
+        out_ref[i * LANES : (i + 1) * LANES, :] = own - 0.5 * product
+
+
+def first_body(cols_ref, tiles_ref, outer_ref, own_ref, inner_ref, out_ref, blocks_ref):
     half = own_ref.shape[0]
     place = lax.axis_index("dev")
-    zeros = jnp.zeros(own_ref.shape, own_ref.dtype)
-    blocks_ref[0:half] = jnp.where(place > 0, before_ref[...], zeros)
+    odd = lax.rem(place, 2) == 1
+    ends = (place == 0) | (place == lax.axis_size("dev") - 1)
+    outer = jnp.where(ends, jnp.zeros(own_ref.shape, own_ref.dtype), outer_ref[...])
     blocks_ref[half : 2 * half] = own_ref[...]
-    blocks_ref[2 * half : 3 * half] = jnp.where(
-        place < lax.axis_size("dev") - 1, after_ref[...], zeros
-    )
+    blocks_ref[pl.ds(jnp.where(odd, 2 * half, 0), half)] = outer
+    blocks_ref[pl.ds(jnp.where(odd, 0, 2 * half), half)] = inner_ref[...]
     product_rows(cols_ref, tiles_ref, blocks_ref, out_ref, 0)
 
 
-def first_rows(cols, tiles, before, own, after, count):
+def first_rows(cols, tiles, outer, own, inner, count):
     half = own.shape[0]
     return pl.pallas_call(
         first_body,
@@ -187,7 +181,7 @@
         out_specs=(VMEM_SPEC, VMEM_SPEC),
         compiler_params=PARAMS,
         name="first_rows",
-    )(cols, tiles, before, own, after)
+    )(cols, tiles, outer, own, inner)
 
 
 def more_body(cols_ref, tiles_ref, blocks_ref, out_ref, *, base):
@@ -236,7 +230,7 @@
 
 
 def per_device(coarse_emb, req_ids, fine_slot, tiles, tile_cols):
-    devices = lax.axis_size("dev")
+    groups, devices = lax.axis_size("grp"), lax.axis_size("dev")
     slots = req_ids.shape[3]
     width = coarse_emb.shape[1]
     row_blocks = tiles.shape[0]
@@ -253,17 +247,20 @@
         wanted.reshape(devices, slots, width), "dev", split_axis=0, concat_axis=0, tiled=True
     )
     lifted = lift((first, second), received.reshape(devices * slots, width))
-    up = [(i, i + 1) for i in range(devices - 1)]
-    down = [((i + 1) % devices, i) for i in range(devices)]
-    before = lax.ppermute(lifted, "dev", up).reshape(-1, LANES, width)
-    after = lax.ppermute(lifted, "dev", down).reshape(-1, LANES, width)
+    inner = [(i, i ^ 1) for i in range(devices)]
+    outer = []
+    for g in range(groups):
+        outer += [(g * devices + i, g * devices + ((i + 1) ^ 1) - 1) for i in range(1, devices - 1)]
+        outer += [(g * devices + i, (g ^ 1) * devices + i) for i in (0, devices - 1)]
+    from_outer = lax.ppermute(lifted, ("grp", "dev"), outer).reshape(-1, LANES, width)
+    from_inner = lax.ppermute(lifted, "dev", inner).reshape(-1, LANES, width)
     own = lifted.reshape(-1, LANES, width)
     cols = tile_cols[:, 0].T
     parts = []
     base = 0
     for c, count in enumerate(CHUNKS):
         if c == 0:
-            mine, blocks = first_rows(cols, tiles, before, own, after, count)
+            mine, blocks = first_rows(cols, tiles, from_outer, own, from_inner, count)
         else:
             mine = more_rows(cols, tiles, blocks, base, count)
         parts.append((mine, lax.ppermute(mine, "grp", [(0, 1), (1, 0)])))

time: 84.8 us -> 82.1 us (0.968)
  the two profiles are of different devices: /device:TPU:3 before, /device:TPU:7 now
where the time goes in v3:
time: 82.1 us; the launch traced here: 81.7 us
  waiting for transfers between devices  34 us (41%)
  starting transfers between devices  30.6 us (37%)
  Pallas kernels  13.2 us (16%)
  local copies, waits for them, and re-layouts  3.76 us (5%)
    all_to_all x1, waiting for transfers between devices, per_device(): lax.all_to_all(wanted.reshape(devices, slots, width), 'dev', split_axis=0...  15.4 us
    all_to_all x1, starting transfers between devices, per_device(): lax.all_to_all(req_ids.reshape(devices, 1, slots), 'dev', split_axis=0, c...  15.3 us
    all_to_all x1, starting transfers between devices, per_device(): lax.all_to_all(wanted.reshape(devices, slots, width), 'dev', split_axis=0...  8.15 us
    all_to_all x1, waiting for transfers between devices, per_device(): lax.all_to_all(req_ids.reshape(devices, 1, slots), 'dev', split_axis=0, c...  6.7 us
    ppermute x1, waiting for transfers between devices, per_device(): lax.ppermute(lifted, ('grp', 'dev'), outer).reshape(-1, LANES, width)  5.02 us
    ppermute x3, starting transfers between devices, per_device(): parts.append((mine, lax.ppermute(mine, 'grp', [(0, 1), (1, 0)])))  4.8 us
    ppermute x1, waiting for transfers between devices, per_device(): from_inner = lax.ppermute(lifted, 'dev', inner).reshape(-1, LANES, width)  4.37 us
    unnamed x9, local copies, waits for them, and re-layouts  3.76 us
  transfers between devices with their start and end apart: 7, of which 5 were waited for; matrix products, arithmetic and copies ran while one was open for 0% of the time, Pallas kernels for 8%

profile of v3, /device:TPU:7, one launch (start us, length us, event | category | flops | bytes accessed | tf_op | source)
XLA Modules:
  0.0 81.7 jit_solution(9546535247731522860)
XLA Ops:
  0.0 1.4 %copy.7 = s32[1,1,128,16]{3,2,1,0:T(8,128)} copy(s32[1,1,128,16]{2,3,1,0:T(8,128)} %param.6) | data formatting | bytes 16384 | tf_op args[1]
  1.4 15.3 %all-to-all-start = ((s32[128,1,16]{2,1,0:T(1,128)}), s32[128,1,16]{2,1,0:T(1,128)S(1)}, u32[]{:S(2)}, u32[]{:S(2)}) async-start(s32[128,1,16]{2,1,0:T(1,128)} %bitcast.5), calls=%async_computation | async-start | bytes 131072 | tf_op jit(solution)/shard_map/all_to_all | solution.py:240
  16.8 0.0 copy-start
  16.8 0.9 %copy-done = bf16[1024,128]{1,0:T(8,128)(2,1)S(1)} copy-done((bf16[1024,128]{1,0:T(8,128)(2,1)S(1)}, bf16[1024,128]{1,0:T(8,128)(2,1)}, u32[]{:S(2)}) %copy-start) | copy-done | bytes 262168
  17.7 0.0 copy-start.2
  17.7 0.7 copy-done.2
  18.4 0.2 columns.2
  18.6 6.7 %all-to-all-done.asked_ref = s32[128,1,16]{2,1,0:T(1,128)S(1)} async-done(((s32[128,1,16]{2,1,0:T(1,128)}), s32[128,1,16]{2,1,0:T(1,128)S(1)}, u32[]{:S(2)}, u32[]{:S(2)}) %all-to-all-start) | async-done | bytes 8224 | tf_op jit(solution)/shard_map/all_to_all | solution.py:240
  25.3 1.6 %gather.1 = bf16[2048,128]{1,0:T(8,128)(2,1)} custom-call(s32[128,1,16]{2,1,0:T(1,128)S(1)} %all-to-all-done.asked_ref, bf16[512,256]{1,0:T(8,128)(2,1)S(1)} %get-tuple-element.10.table_ref), custom_call_target="tpu_custom_call" | custom-call | tf_op jit(solution)/shard_map/gather/pallas_call | solution.py:60
  27.0 8.1 %all-to-all-start.1 = ((bf16[128,16,128]{2,1,0:T(8,128)(2,1)}), bf16[128,16,128]{2,1,0:T(8,128)(2,1)S(1)}, u32[]{:S(2)}, u32[]{:S(2)}) async-start(bf16[128,16,128]{2,1,0:T(8,128)(2,1)} %bitcast.6), calls=%async_computation.1 | async-start | bytes 1048576 | tf_op jit(solution)/shard_map/all_to_all | solution.py:246
  35.1 0.0 copy-start.3
  35.1 0.7 copy-done.3
  35.8 0.2 columns.3.refs_1_
  36.0 15.4 %all-to-all-done.1 = bf16[128,16,128]{2,1,0:T(8,128)(2,1)S(1)} async-done(((bf16[128,16,128]{2,1,0:T(8,128)(2,1)}), bf16[128,16,128]{2,1,0:T(8,128)(2,1)S(1)}, u32[]{:S(2)}, u32[]{:S(2)}) %all-to-all-start.1) | async-done | bytes 524320 | tf_op jit(solution)/shard_map/all_to_all | solution.py:246
  51.4 1.3 %lift.1 = bf16[2048,128]{1,0:T(8,128)(2,1)S(1)} custom-call(s32[1024,128]{1,0:T(8,128)S(1)} %get-tuple-element.9.refs_0_, s32[1024,128]{1,0:T(8,128)S(1)} %columns.3.refs_1_, bf16[2048,128]{1,0:T(8,128)(2,1)S(1)} %bitcast.12), custom_call_target="tpu_custom_call" | custom-call | tf_op jit(solution)/shard_map/lift/pallas_call | solution.py:108
  52.7 0.8 collective-permute-start.1
  53.5 1.5 %collective-permute-start = (bf16[2048,128]{1,0:T(8,128)(2,1)S(1)}, bf16[2048,128]{1,0:T(8,128)(2,1)S(1)}, u32[]{:S(2)}, u32[]{:S(2)}) collective-permute-start(bf16[2048,128]{1,0:T(8,128)(2,1)S(1)} %lift.1), channel_id=1, source_target_pairs={{1,2},{2,1},{3,4},{4,3},{5,6},{6,5},{7,8},{8,7},{9,10},{10,9},{11,... | collective-permute-start | bytes 1572872 | tf_op jit(solution)/shard_map/ppermute | solution.py:255
  55.0 3.5 %load.1.tiles_ref = bf16[32,8,128,128]{3,2,1,0:T(8,128)(2,1)S(1)} custom-call(bf16[32,8,128,128]{3,2,1,0:T(8,128)(2,1)} %bitcast.20), custom_call_target="tpu_custom_call" | custom-call | tf_op jit(solution)/shard_map/load/pallas_call | solution.py:133
  58.5 4.4 %collective-permute-done.1 = bf16[2048,128]{1,0:T(8,128)(2,1)S(1)} collective-permute-done((bf16[2048,128]{1,0:T(8,128)(2,1)S(1)}, bf16[2048,128]{1,0:T(8,128)(2,1)S(1)}, u32[]{:S(2)}, u32[]{:S(2)}) %collective-permute-start.1) | collective-permute-done | bytes 524320 | tf_op jit(solution)/shard_map/ppermute | solution.py:256
  62.9 5.0 %collective-permute-done = bf16[2048,128]{1,0:T(8,128)(2,1)S(1)} collective-permute-done((bf16[2048,128]{1,0:T(8,128)(2,1)S(1)}, bf16[2048,128]{1,0:T(8,128)(2,1)S(1)}, u32[]{:S(2)}, u32[]{:S(2)}) %collective-permute-start) | collective-permute-done | bytes 524320 | tf_op jit(solution)/shard_map/ppermute | solution.py:255
  67.9 0.0 copy-done.1
  67.9 1.5 %first_rows.1 = (f32[1024,128]{1,0:T(8,128)S(1)}, bf16[48,128,128]{2,1,0:T(8,128)(2,1)S(1)}) custom-call(s32[8,32]{1,0:T(8,128)S(1)} %bitcast.15, bf16[32,8,128,128]{3,2,1,0:T(8,128)(2,1)S(1)} %load.1.tiles_ref, bf16[16,128,128]{2,1,0:T(8,128)(2,1)S(1)} %bitcast.14, bf16[16,128,128]{2,1,0:T(8,128)(2,1)S(1)} %bitcast.11, bf16[16,128,128]{2,1,0:T(8,128)(2,1)S(1)} %bitcast.13), custom_call_target="tpu_custom_call" | custom-call | tf_op jit(solution)/shard_map/first_rows/pallas_call | solution.py:174
  69.4 1.6 %more_rows.3.refs_2_ = f32[1536,128]{1,0:T(8,128)S(1)} custom-call(s32[8,32]{1,0:T(8,128)S(1)} %bitcast.16, bf16[32,8,128,128]{3,2,1,0:T(8,128)(2,1)S(1)} %load.1.tiles_ref, bf16[48,128,128]{2,1,0:T(8,128)(2,1)S(1)} %get-tuple-element.11.blocks_ref), custom_call_target="tpu_custom_call" | custom-call | tf_op jit(solution)/shard_map/more_rows/pallas_call | solution.py:192
  71.0 4.2 %collective-permute-start.4 = (f32[1536,128]{1,0:T(8,128)S(1)}, f32[1536,128]{1,0:T(8,128)S(1)}, u32[]{:S(2)}, u32[]{:S(2)}) collective-permute-start(f32[1536,128]{1,0:T(8,128)S(1)} %more_rows.3.refs_2_), channel_id=1, source_target_pairs={{0,128},{128,0},{1,129},{129,1},{2,130},{130,2},{3,131},{131,3},{4... | collective-permute-start | bytes 2359304 | tf_op jit(solution)/shard_map/ppermute | solution.py:266
  75.2 1.6 %more_rows.2.refs_0_ = f32[1536,128]{1,0:T(8,128)S(1)} custom-call(s32[8,32]{1,0:T(8,128)S(1)} %bitcast.17, bf16[32,8,128,128]{3,2,1,0:T(8,128)(2,1)S(1)} %load.1.tiles_ref, bf16[48,128,128]{2,1,0:T(8,128)(2,1)S(1)} %get-tuple-element.11.blocks_ref), custom_call_target="tpu_custom_call" | custom-call | tf_op jit(solution)/shard_map/more_rows/pallas_call | solution.py:192
  76.8 0.1 collective-permute-start.2
  76.9 0.5 collective-permute-start.3
  77.4 2.5 %collective-permute-done.3.refs_1_ = f32[1024,128]{1,0:T(8,128)S(1)} collective-permute-done((f32[1024,128]{1,0:T(8,128)S(1)}, f32[1024,128]{1,0:T(8,128)S(1)}, u32[]{:S(2)}, u32[]{:S(2)}) %collective-permute-start.3) | collective-permute-done | bytes 524320 | tf_op jit(solution)/shard_map/ppermute | solution.py:266
  79.9 0.0 collective-permute-done.4.refs_3_
  79.9 1.0 %combine.2.refs_2_ = bf16[4096,128]{1,0:T(8,128)(2,1)} custom-call(f32[1024,128]{1,0:T(8,128)S(1)} %get-tuple-element.12.refs_0_, f32[1024,128]{1,0:T(8,128)S(1)} %collective-permute-done.3.refs_1_, f32[1536,128]{1,0:T(8,128)S(1)} %more_rows.3.refs_2_, f32[1536,128]{1,0:T(8,128)S(1)} %collective-permute-done.4.refs_3_), custom_call_target="tpu_custom_call" | custom-call | tf_op jit(solution)/shard_map/combine/pallas_call | solution.py:220
  80.9 0.0 collective-permute-done.2.refs_1_
  80.9 0.8 %combine.3 = bf16[4096,128]{1,0:T(8,128)(2,1)} custom-call(f32[1536,128]{1,0:T(8,128)S(1)} %more_rows.2.refs_0_, f32[1536,128]{1,0:T(8,128)S(1)} %collective-permute-done.2.refs_1_, bf16[4096,128]{1,0:T(8,128)(2,1)} %combine.2.refs_2_), custom_call_target="tpu_custom_call", output_to_operand_aliasing={{}: (2, {})} | custom-call | tf_op jit(solution)/shard_map/combine/pallas_call | solution.py:220
  (1 shorter events, 0.0 us)
Async XLA Ops:
  1.4 23.9 %all-to-all-start = ((s32[128,1,16]{2,1,0:T(1,128)}), s32[128,1,16]{2,1,0:T(1,128)S(1)}, u32[]{:S(2)}, u32[]{:S(2)}) async-start(s32[128,1,16]{2,1,0:T(1,128)} %bitcast.5), calls=%async_computation | async-start | bytes 131072 | tf_op jit(solution)/shard_map/all_to_all | solution.py:240
  16.8 1.0 %copy-start = (bf16[1024,128]{1,0:T(8,128)(2,1)S(1)}, bf16[1024,128]{1,0:T(8,128)(2,1)}, u32[]{:S(2)}) copy-start(bf16[1024,128]{1,0:T(8,128)(2,1)} %refs_0_.1) | copy-start | bytes 786436
  17.7 0.7 copy-start.2
  27.0 24.5 %all-to-all-start.1 = ((bf16[128,16,128]{2,1,0:T(8,128)(2,1)}), bf16[128,16,128]{2,1,0:T(8,128)(2,1)S(1)}, u32[]{:S(2)}, u32[]{:S(2)}) async-start(bf16[128,16,128]{2,1,0:T(8,128)(2,1)} %bitcast.6), calls=%async_computation.1 | async-start | bytes 1048576 | tf_op jit(solution)/shard_map/all_to_all | solution.py:246
  35.1 0.7 copy-start.3
  52.7 10.2 %collective-permute-start.1 = (bf16[2048,128]{1,0:T(8,128)(2,1)S(1)}, bf16[2048,128]{1,0:T(8,128)(2,1)S(1)}, u32[]{:S(2)}, u32[]{:S(2)}) collective-permute-start(bf16[2048,128]{1,0:T(8,128)(2,1)S(1)} %lift.1), channel_id=1, source_target_pairs={{0,1},{1,0},{2,3},{3,2},{4,5},{5,4},{6,7},{7,6},{8,9},{9,8},{10,11... | collective-permute-start | bytes 1572872 | tf_op jit(solution)/shard_map/ppermute | solution.py:256
  53.5 14.4 %collective-permute-start = (bf16[2048,128]{1,0:T(8,128)(2,1)S(1)}, bf16[2048,128]{1,0:T(8,128)(2,1)S(1)}, u32[]{:S(2)}, u32[]{:S(2)}) collective-permute-start(bf16[2048,128]{1,0:T(8,128)(2,1)S(1)} %lift.1), channel_id=1, source_target_pairs={{1,2},{2,1},{3,4},{4,3},{5,6},{6,5},{7,8},{8,7},{9,10},{10,9},{11,... | collective-permute-start | bytes 1572872 | tf_op jit(solution)/shard_map/ppermute | solution.py:255
  55.0 12.9 %copy-start.1 = (s32[32,1,8]{0,2,1:T(8,128)S(1)}, s32[32,1,8]{0,2,1:T(8,128)}, u32[]{:S(2)}) copy-start(s32[32,1,8]{0,2,1:T(8,128)} %param.9) | copy-start | bytes 3076
  71.0 8.9 %collective-permute-start.4 = (f32[1536,128]{1,0:T(8,128)S(1)}, f32[1536,128]{1,0:T(8,128)S(1)}, u32[]{:S(2)}, u32[]{:S(2)}) collective-permute-start(f32[1536,128]{1,0:T(8,128)S(1)} %more_rows.3.refs_2_), channel_id=1, source_target_pairs={{0,128},{128,0},{1,129},{129,1},{2,130},{130,2},{3,131},{131,3},{4... | collective-permute-start | bytes 2359304 | tf_op jit(solution)/shard_map/ppermute | solution.py:266
  76.8 4.1 %collective-permute-start.2 = (f32[1536,128]{1,0:T(8,128)S(1)}, f32[1536,128]{1,0:T(8,128)S(1)}, u32[]{:S(2)}, u32[]{:S(2)}) collective-permute-start(f32[1536,128]{1,0:T(8,128)S(1)} %more_rows.2.refs_0_), channel_id=1, source_target_pairs={{0,128},{128,0},{1,129},{129,1},{2,130},{130,2},{3,131},{131,3},{4... | collective-permute-start | bytes 2359304 | tf_op jit(solution)/shard_map/ppermute | solution.py:266
  76.9 3.0 %collective-permute-start.3 = (f32[1024,128]{1,0:T(8,128)S(1)}, f32[1024,128]{1,0:T(8,128)S(1)}, u32[]{:S(2)}, u32[]{:S(2)}) collective-permute-start(f32[1024,128]{1,0:T(8,128)S(1)} %get-tuple-element.12.refs_0_), channel_id=1, source_target_pairs={{0,128},{128,0},{1,129},{129,1},{2,130},{130,2},{3,131},{131,3},{4... | collective-permute-start | bytes 1572872 | tf_op jit(solution)/shard_map/ppermute | solution.py:266

commit v4 on v3

--- a/solution.py
+++ b/solution.py
@@ -115,7 +115,7 @@
     )(*parts, table)
 
 
-def load_body(tiles_ref, out_ref, sems, *, pieces):
+def load_body(tiles_ref, cols_ref, out_ref, cols_out_ref, sems, *, pieces):
     each = tiles_ref.shape[0] // pieces
     copies = [
         pltpu.make_async_copy(
@@ -123,22 +123,23 @@
         )
         for p in range(pieces)
     ]
+    copies.append(pltpu.make_async_copy(cols_ref, cols_out_ref, sems.at[pieces]))
     for copy in copies:
         copy.start()
     for copy in copies:
         copy.wait()
 
 
-def load(tiles):
+def load(tiles, cols):
     return pl.pallas_call(
         functools.partial(load_body, pieces=4),
-        out_shape=pltpu.VMEM(tiles.shape, tiles.dtype),
-        in_specs=[pl.BlockSpec(memory_space=pltpu.HBM)],
-        out_specs=VMEM_SPEC,
-        scratch_shapes=[pltpu.SemaphoreType.DMA((4,))],
+        out_shape=(pltpu.VMEM(tiles.shape, tiles.dtype), pltpu.SMEM(cols.shape, cols.dtype)),
+        in_specs=[pl.BlockSpec(memory_space=pltpu.HBM)] * 2,
+        out_specs=(VMEM_SPEC, SMEM_SPEC),
+        scratch_shapes=[pltpu.SemaphoreType.DMA((5,))],
         compiler_params=pltpu.CompilerParams(vmem_limit_bytes=48 * 1024 * 1024),
         name="load",
-    )(tiles)
+    )(tiles, cols)
 
 
 def product_rows(cols_ref, tiles_ref, blocks_ref, out_ref, base):
@@ -236,7 +237,7 @@
     row_blocks = tiles.shape[0]
     index = fine_slot.reshape(-1, LANES)
     half = index.shape[0] // 2
-    tiles = load(tiles[:, 0])
+    tiles, cols = load(tiles[:, 0], tile_cols[:, 0].T)
     asked = lax.all_to_all(
         req_ids.reshape(devices, 1, slots), "dev", split_axis=0, concat_axis=0, tiled=True
     )
@@ -255,7 +256,6 @@
     from_outer = lax.ppermute(lifted, ("grp", "dev"), outer).reshape(-1, LANES, width)
     from_inner = lax.ppermute(lifted, "dev", inner).reshape(-1, LANES, width)
     own = lifted.reshape(-1, LANES, width)
-    cols = tile_cols[:, 0].T
     parts = []
     base = 0
     for c, count in enumerate(CHUNKS):
@@ -266,8 +266,11 @@
         parts.append((mine, lax.ppermute(mine, "grp", [(0, 1), (1, 0)])))
         base += count
     rows = row_blocks * LANES
-    out = combine(parts[:-1], None, rows, 0, lifted.dtype)
-    return combine(parts[-1:], out, rows, rows - parts[-1][0].shape[0], lifted.dtype)
+    out, base = None, 0
+    for part in parts:
+        out = combine([part], out, rows, base, lifted.dtype)
+        base += part[0].shape[0]
+    return out
 
 
 def solution(mesh):

time: 82.1 us -> 80.9 us (0.985)
  Pallas kernels: 13.2 us -> 12 us
    pallas_call x2, Pallas kernels: 3.17 us -> 1.95 us  [more_rows(): pl.pallas_call(functools.partial(more_body, base=base), out_shape=jax.Sha...]
    pallas_call x2 -> x3, Pallas kernels: 1.79 us -> 2.41 us  [combine(): pl.pallas_call(functools.partial(combine_body, first=first), out_shape=ja...]
    unnamed x9 -> x7, local copies, waits for them, and re-layouts: 3.76 us -> 3.76 us
where the time goes in v4:
time: 80.9 us; the launch traced here: 80.5 us
  waiting for transfers between devices  34 us (42%)
  starting transfers between devices  30.6 us (38%)
  Pallas kernels  12 us (15%)
  local copies, waits for them, and re-layouts  3.76 us (5%)
    all_to_all x1, waiting for transfers between devices, per_device(): lax.all_to_all(wanted.reshape(devices, slots, width), 'dev', split_axis=0...  15.4 us
    all_to_all x1, starting transfers between devices, per_device(): lax.all_to_all(req_ids.reshape(devices, 1, slots), 'dev', split_axis=0, c...  15.3 us
    all_to_all x1, starting transfers between devices, per_device(): lax.all_to_all(wanted.reshape(devices, slots, width), 'dev', split_axis=0...  8.15 us
    all_to_all x1, waiting for transfers between devices, per_device(): lax.all_to_all(req_ids.reshape(devices, 1, slots), 'dev', split_axis=0, c...  6.7 us
    ppermute x1, waiting for transfers between devices, per_device(): lax.ppermute(lifted, ('grp', 'dev'), outer).reshape(-1, LANES, width)  5.02 us
    ppermute x3, starting transfers between devices, per_device(): parts.append((mine, lax.ppermute(mine, 'grp', [(0, 1), (1, 0)])))  4.8 us
    ppermute x1, waiting for transfers between devices, per_device(): from_inner = lax.ppermute(lifted, 'dev', inner).reshape(-1, LANES, width)  4.37 us
    unnamed x7, local copies, waits for them, and re-layouts  3.76 us
  transfers between devices with their start and end apart: 7, of which 5 were waited for; matrix products, arithmetic and copies ran while one was open for 0% of the time, Pallas kernels for 8%

profile of v4, /device:TPU:7, one launch (start us, length us, event | category | flops | bytes accessed | tf_op | source)
XLA Modules:
  0.0 80.5 jit_solution(9964079430416181086)
XLA Ops:
  0.0 1.4 %copy.8 = s32[1,1,128,16]{3,2,1,0:T(8,128)} copy(s32[1,1,128,16]{2,3,1,0:T(8,128)} %param.6) | data formatting | bytes 16384 | tf_op args[1]
  1.4 15.3 %all-to-all-start = ((s32[128,1,16]{2,1,0:T(1,128)}), s32[128,1,16]{2,1,0:T(1,128)S(1)}, u32[]{:S(2)}, u32[]{:S(2)}) async-start(s32[128,1,16]{2,1,0:T(1,128)} %bitcast.4), calls=%async_computation | async-start | bytes 131072 | tf_op jit(solution)/shard_map/all_to_all | solution.py:241
  16.8 0.0 copy-start
  16.8 0.9 %copy-done = bf16[1024,128]{1,0:T(8,128)(2,1)S(1)} copy-done((bf16[1024,128]{1,0:T(8,128)(2,1)S(1)}, bf16[1024,128]{1,0:T(8,128)(2,1)}, u32[]{:S(2)}) %copy-start) | copy-done | bytes 262168
  17.7 0.0 copy-start.1
  17.7 0.7 copy-done.1
  18.4 0.2 columns.2
  18.6 6.7 %all-to-all-done.asked_ref = s32[128,1,16]{2,1,0:T(1,128)S(1)} async-done(((s32[128,1,16]{2,1,0:T(1,128)}), s32[128,1,16]{2,1,0:T(1,128)S(1)}, u32[]{:S(2)}, u32[]{:S(2)}) %all-to-all-start) | async-done | bytes 8224 | tf_op jit(solution)/shard_map/all_to_all | solution.py:241
  25.3 1.6 %gather.1 = bf16[2048,128]{1,0:T(8,128)(2,1)} custom-call(s32[128,1,16]{2,1,0:T(1,128)S(1)} %all-to-all-done.asked_ref, bf16[512,256]{1,0:T(8,128)(2,1)S(1)} %get-tuple-element.14.table_ref), custom_call_target="tpu_custom_call" | custom-call | tf_op jit(solution)/shard_map/gather/pallas_call | solution.py:60
  27.0 8.1 %all-to-all-start.1 = ((bf16[128,16,128]{2,1,0:T(8,128)(2,1)}), bf16[128,16,128]{2,1,0:T(8,128)(2,1)S(1)}, u32[]{:S(2)}, u32[]{:S(2)}) async-start(bf16[128,16,128]{2,1,0:T(8,128)(2,1)} %bitcast.5), calls=%async_computation.1 | async-start | bytes 1048576 | tf_op jit(solution)/shard_map/all_to_all | solution.py:247
  35.1 0.0 copy-start.2
  35.1 0.7 copy-done.2
  35.8 0.2 columns.3.refs_1_
  36.0 15.4 %all-to-all-done.1 = bf16[128,16,128]{2,1,0:T(8,128)(2,1)S(1)} async-done(((bf16[128,16,128]{2,1,0:T(8,128)(2,1)}), bf16[128,16,128]{2,1,0:T(8,128)(2,1)S(1)}, u32[]{:S(2)}, u32[]{:S(2)}) %all-to-all-start.1) | async-done | bytes 524320 | tf_op jit(solution)/shard_map/all_to_all | solution.py:247
  51.4 1.3 %lift.1 = bf16[2048,128]{1,0:T(8,128)(2,1)S(1)} custom-call(s32[1024,128]{1,0:T(8,128)S(1)} %get-tuple-element.13.refs_0_, s32[1024,128]{1,0:T(8,128)S(1)} %columns.3.refs_1_, bf16[2048,128]{1,0:T(8,128)(2,1)S(1)} %bitcast.12), custom_call_target="tpu_custom_call" | custom-call | tf_op jit(solution)/shard_map/lift/pallas_call | solution.py:108
  52.7 0.8 collective-permute-start.1
  53.5 1.5 %collective-permute-start = (bf16[2048,128]{1,0:T(8,128)(2,1)S(1)}, bf16[2048,128]{1,0:T(8,128)(2,1)S(1)}, u32[]{:S(2)}, u32[]{:S(2)}) collective-permute-start(bf16[2048,128]{1,0:T(8,128)(2,1)S(1)} %lift.1), channel_id=1, source_target_pairs={{1,2},{2,1},{3,4},{4,3},{5,6},{6,5},{7,8},{8,7},{9,10},{10,9},{11,... | collective-permute-start | bytes 1572872 | tf_op jit(solution)/shard_map/ppermute | solution.py:256
  55.0 3.5 %load.1 = (bf16[32,8,128,128]{3,2,1,0:T(8,128)(2,1)S(1)}, s32[8,32]{1,0:T(8,128)S(4)}) custom-call(bf16[32,8,128,128]{3,2,1,0:T(8,128)(2,1)} %bitcast.17, s32[8,32]{1,0:T(8,128)} %bitcast.18), custom_call_target="tpu_custom_call" | custom-call | tf_op jit(solution)/shard_map/load/pallas_call | solution.py:134
  58.5 4.4 %collective-permute-done.1 = bf16[2048,128]{1,0:T(8,128)(2,1)S(1)} collective-permute-done((bf16[2048,128]{1,0:T(8,128)(2,1)S(1)}, bf16[2048,128]{1,0:T(8,128)(2,1)S(1)}, u32[]{:S(2)}, u32[]{:S(2)}) %collective-permute-start.1) | collective-permute-done | bytes 524320 | tf_op jit(solution)/shard_map/ppermute | solution.py:257
  62.9 5.0 %collective-permute-done = bf16[2048,128]{1,0:T(8,128)(2,1)S(1)} collective-permute-done((bf16[2048,128]{1,0:T(8,128)(2,1)S(1)}, bf16[2048,128]{1,0:T(8,128)(2,1)S(1)}, u32[]{:S(2)}, u32[]{:S(2)}) %collective-permute-start) | collective-permute-done | bytes 524320 | tf_op jit(solution)/shard_map/ppermute | solution.py:256
  67.9 0.9 %first_rows.1 = (f32[1024,128]{1,0:T(8,128)S(1)}, bf16[48,128,128]{2,1,0:T(8,128)(2,1)S(1)}) custom-call(s32[8,32]{1,0:T(8,128)S(4)} %get-tuple-element.11.cols_ref, bf16[32,8,128,128]{3,2,1,0:T(8,128)(2,1)S(1)} %get-tuple-element.12.tiles_ref, bf16[16,128,128]{2,1,0:T(8,128)(2,1)S(1)} %bitcast.14, bf16[16,128,128]{2,1,0:T(8,128)(2,1)S(1)} %bitcast.11, ...), custom_call_target="tpu_custom_call" | custom-call | tf_op jit(solution)/shard_map/first_rows/pallas_call | solution.py:175
  68.8 1.0 %more_rows.3.refs_0_ = f32[1536,128]{1,0:T(8,128)S(1)} custom-call(s32[8,32]{1,0:T(8,128)S(4)} %get-tuple-element.11.cols_ref, bf16[32,8,128,128]{3,2,1,0:T(8,128)(2,1)S(1)} %get-tuple-element.12.tiles_ref, bf16[48,128,128]{2,1,0:T(8,128)(2,1)S(1)} %get-tuple-element.15.blocks_ref), custom_call_target="tpu_custom_call" | custom-call | tf_op jit(solution)/shard_map/more_rows/pallas_call | solution.py:193
  69.8 4.2 %collective-permute-start.3 = (f32[1536,128]{1,0:T(8,128)S(1)}, f32[1536,128]{1,0:T(8,128)S(1)}, u32[]{:S(2)}, u32[]{:S(2)}) collective-permute-start(f32[1536,128]{1,0:T(8,128)S(1)} %more_rows.3.refs_0_), channel_id=1, source_target_pairs={{0,128},{128,0},{1,129},{129,1},{2,130},{130,2},{3,131},{131,3},{4... | collective-permute-start | bytes 2359304 | tf_op jit(solution)/shard_map/ppermute | solution.py:266
  74.0 1.0 %more_rows.2.refs_0_ = f32[1536,128]{1,0:T(8,128)S(1)} custom-call(s32[8,32]{1,0:T(8,128)S(4)} %get-tuple-element.11.cols_ref, bf16[32,8,128,128]{3,2,1,0:T(8,128)(2,1)S(1)} %get-tuple-element.12.tiles_ref, bf16[48,128,128]{2,1,0:T(8,128)(2,1)S(1)} %get-tuple-element.15.blocks_ref), custom_call_target="tpu_custom_call" | custom-call | tf_op jit(solution)/shard_map/more_rows/pallas_call | solution.py:193
  74.9 0.1 collective-permute-start.2
  75.0 0.5 collective-permute-start.4
  75.5 2.5 %collective-permute-done.4.refs_1_ = f32[1024,128]{1,0:T(8,128)S(1)} collective-permute-done((f32[1024,128]{1,0:T(8,128)S(1)}, f32[1024,128]{1,0:T(8,128)S(1)}, u32[]{:S(2)}, u32[]{:S(2)}) %collective-permute-start.4) | collective-permute-done | bytes 524320 | tf_op jit(solution)/shard_map/ppermute | solution.py:266
  78.1 0.8 combine.3.refs_2_
  78.8 0.0 collective-permute-done.3.refs_1_
  78.8 0.8 %combine.4.refs_2_ = bf16[4096,128]{1,0:T(8,128)(2,1)} custom-call(f32[1536,128]{1,0:T(8,128)S(1)} %more_rows.3.refs_0_, f32[1536,128]{1,0:T(8,128)S(1)} %collective-permute-done.3.refs_1_, bf16[4096,128]{1,0:T(8,128)(2,1)} %combine.3.refs_2_), custom_call_target="tpu_custom_call", output_to_operand_aliasing={{}: (2, {})} | custom-call | tf_op jit(solution)/shard_map/combine/pallas_call | solution.py:221
  79.7 0.0 collective-permute-done.2.refs_1_
  79.7 0.8 %combine.5 = bf16[4096,128]{1,0:T(8,128)(2,1)} custom-call(f32[1536,128]{1,0:T(8,128)S(1)} %more_rows.2.refs_0_, f32[1536,128]{1,0:T(8,128)S(1)} %collective-permute-done.2.refs_1_, bf16[4096,128]{1,0:T(8,128)(2,1)} %combine.4.refs_2_), custom_call_target="tpu_custom_call", output_to_operand_aliasing={{}: (2, {})} | custom-call | tf_op jit(solution)/shard_map/combine/pallas_call | solution.py:221
Async XLA Ops:
  1.4 23.9 %all-to-all-start = ((s32[128,1,16]{2,1,0:T(1,128)}), s32[128,1,16]{2,1,0:T(1,128)S(1)}, u32[]{:S(2)}, u32[]{:S(2)}) async-start(s32[128,1,16]{2,1,0:T(1,128)} %bitcast.4), calls=%async_computation | async-start | bytes 131072 | tf_op jit(solution)/shard_map/all_to_all | solution.py:241
  16.8 1.0 %copy-start = (bf16[1024,128]{1,0:T(8,128)(2,1)S(1)}, bf16[1024,128]{1,0:T(8,128)(2,1)}, u32[]{:S(2)}) copy-start(bf16[1024,128]{1,0:T(8,128)(2,1)} %refs_0_.1) | copy-start | bytes 786436
  17.7 0.7 copy-start.1
  27.0 24.5 %all-to-all-start.1 = ((bf16[128,16,128]{2,1,0:T(8,128)(2,1)}), bf16[128,16,128]{2,1,0:T(8,128)(2,1)S(1)}, u32[]{:S(2)}, u32[]{:S(2)}) async-start(bf16[128,16,128]{2,1,0:T(8,128)(2,1)} %bitcast.5), calls=%async_computation.1 | async-start | bytes 1048576 | tf_op jit(solution)/shard_map/all_to_all | solution.py:247
  35.1 0.7 copy-start.2
  52.7 10.2 %collective-permute-start.1 = (bf16[2048,128]{1,0:T(8,128)(2,1)S(1)}, bf16[2048,128]{1,0:T(8,128)(2,1)S(1)}, u32[]{:S(2)}, u32[]{:S(2)}) collective-permute-start(bf16[2048,128]{1,0:T(8,128)(2,1)S(1)} %lift.1), channel_id=1, source_target_pairs={{0,1},{1,0},{2,3},{3,2},{4,5},{5,4},{6,7},{7,6},{8,9},{9,8},{10,11... | collective-permute-start | bytes 1572872 | tf_op jit(solution)/shard_map/ppermute | solution.py:257
  53.5 14.4 %collective-permute-start = (bf16[2048,128]{1,0:T(8,128)(2,1)S(1)}, bf16[2048,128]{1,0:T(8,128)(2,1)S(1)}, u32[]{:S(2)}, u32[]{:S(2)}) collective-permute-start(bf16[2048,128]{1,0:T(8,128)(2,1)S(1)} %lift.1), channel_id=1, source_target_pairs={{1,2},{2,1},{3,4},{4,3},{5,6},{6,5},{7,8},{8,7},{9,10},{10,9},{11,... | collective-permute-start | bytes 1572872 | tf_op jit(solution)/shard_map/ppermute | solution.py:256
  69.8 9.1 %collective-permute-start.3 = (f32[1536,128]{1,0:T(8,128)S(1)}, f32[1536,128]{1,0:T(8,128)S(1)}, u32[]{:S(2)}, u32[]{:S(2)}) collective-permute-start(f32[1536,128]{1,0:T(8,128)S(1)} %more_rows.3.refs_0_), channel_id=1, source_target_pairs={{0,128},{128,0},{1,129},{129,1},{2,130},{130,2},{3,131},{131,3},{4... | collective-permute-start | bytes 2359304 | tf_op jit(solution)/shard_map/ppermute | solution.py:266
  74.9 4.7 %collective-permute-start.2 = (f32[1536,128]{1,0:T(8,128)S(1)}, f32[1536,128]{1,0:T(8,128)S(1)}, u32[]{:S(2)}, u32[]{:S(2)}) collective-permute-start(f32[1536,128]{1,0:T(8,128)S(1)} %more_rows.2.refs_0_), channel_id=1, source_target_pairs={{0,128},{128,0},{1,129},{129,1},{2,130},{130,2},{3,131},{131,3},{4... | collective-permute-start | bytes 2359304 | tf_op jit(solution)/shard_map/ppermute | solution.py:266
  75.0 3.0 %collective-permute-start.4 = (f32[1024,128]{1,0:T(8,128)S(1)}, f32[1024,128]{1,0:T(8,128)S(1)}, u32[]{:S(2)}, u32[]{:S(2)}) collective-permute-start(f32[1024,128]{1,0:T(8,128)S(1)} %get-tuple-element.16.refs_0_), channel_id=1, source_target_pairs={{0,128},{128,0},{1,129},{129,1},{2,130},{130,2},{3,131},{131,3},{4... | collective-permute-start | bytes 1572872 | tf_op jit(solution)/shard_map/ppermute | solution.py:266

commit v5 on v4

--- a/solution.py
+++ b/solution.py
@@ -241,13 +241,12 @@
     asked = lax.all_to_all(
         req_ids.reshape(devices, 1, slots), "dev", split_axis=0, concat_axis=0, tiled=True
     )
-    table, first = columns(index, 0, half, coarse_emb)
+    table, first = columns(index, 0, 2 * half, coarse_emb)
     wanted = gather(asked, table)
-    (second,) = columns(index, half, half)
     received = lax.all_to_all(
         wanted.reshape(devices, slots, width), "dev", split_axis=0, concat_axis=0, tiled=True
     )
-    lifted = lift((first, second), received.reshape(devices * slots, width))
+    lifted = lift((first,), received.reshape(devices * slots, width))
     inner = [(i, i ^ 1) for i in range(devices)]
     outer = []
     for g in range(groups):

time: 80.9 us -> 79.2 us (0.979)
  blocking collectives: 0 us -> 23.7 us
  waiting for transfers between devices: 34 us -> 18.4 us
  starting transfers between devices: 30.6 us -> 22.5 us
    all_to_all x0 -> x1, blocking collectives: none -> 23.7 us  [per_device(): lax.all_to_all(wanted.reshape(devices, slots, width), 'dev', split_axis=0...]
    all_to_all x1 -> x0, waiting for transfers between devices: 15.4 us -> none  [per_device(): lax.all_to_all(wanted.reshape(devices, slots, width), 'dev', split_axis=0...]
    all_to_all x1 -> x0, starting transfers between devices: 8.15 us -> none  [per_device(): lax.all_to_all(wanted.reshape(devices, slots, width), 'dev', split_axis=0...]
    unnamed x7 -> x5, local copies, waits for them, and re-layouts: 3.76 us -> 3.07 us
  transfers between devices with their start and end apart: 7 -> 6, of which waited for: 5 -> 4; matrix products, arithmetic and copies ran while one was open for 0% -> 0% of each run, Pallas kernels for 8% -> 8%
where the time goes in v5:
time: 79.2 us; the launch traced here: 78.9 us
  blocking collectives  23.7 us (30%)
  starting transfers between devices  22.5 us (28%)
  waiting for transfers between devices  18.4 us (23%)
  Pallas kernels  11.2 us (14%)
  local copies, waits for them, and re-layouts  3.07 us (4%)
    all_to_all x1, blocking collectives, per_device(): lax.all_to_all(wanted.reshape(devices, slots, width), 'dev', split_axis=0...  23.7 us
    all_to_all x1, starting transfers between devices, per_device(): lax.all_to_all(req_ids.reshape(devices, 1, slots), 'dev', split_axis=0, c...  15.3 us
    all_to_all x1, waiting for transfers between devices, per_device(): lax.all_to_all(req_ids.reshape(devices, 1, slots), 'dev', split_axis=0, c...  6.57 us
    ppermute x3, starting transfers between devices, per_device(): parts.append((mine, lax.ppermute(mine, 'grp', [(0, 1), (1, 0)])))  4.95 us
    ppermute x1, waiting for transfers between devices, per_device(): lax.ppermute(lifted, ('grp', 'dev'), outer).reshape(-1, LANES, width)  4.84 us
    ppermute x1, waiting for transfers between devices, per_device(): from_inner = lax.ppermute(lifted, 'dev', inner).reshape(-1, LANES, width)  4.42 us
    pallas_call x1, Pallas kernels, load(): pl.pallas_call(functools.partial(load_body, pieces=4), out_shape=(pltpu.V...  3.52 us
    unnamed x5, local copies, waits for them, and re-layouts  3.07 us
  transfers between devices with their start and end apart: 6, of which 4 were waited for; matrix products, arithmetic and copies ran while one was open for 0% of the time, Pallas kernels for 8%

profile of v5, /device:TPU:7, one launch (start us, length us, event | category | flops | bytes accessed | tf_op | source)
XLA Modules:
  0.0 78.9 jit_solution(14705068525653236691)
XLA Ops:
  0.0 1.4 %copy.8 = s32[1,1,128,16]{3,2,1,0:T(8,128)} copy(s32[1,1,128,16]{2,3,1,0:T(8,128)} %param.6) | data formatting | bytes 16384 | tf_op args[1]
  1.4 15.3 %all-to-all-start = ((s32[128,1,16]{2,1,0:T(1,128)}), s32[128,1,16]{2,1,0:T(1,128)S(1)}, u32[]{:S(2)}, u32[]{:S(2)}) async-start(s32[128,1,16]{2,1,0:T(1,128)} %bitcast.4), calls=%async_computation | async-start | bytes 131072 | tf_op jit(solution)/shard_map/all_to_all | solution.py:241
  16.8 0.0 copy-start
  16.8 0.9 %copy-done = bf16[1024,128]{1,0:T(8,128)(2,1)S(1)} copy-done((bf16[1024,128]{1,0:T(8,128)(2,1)S(1)}, bf16[1024,128]{1,0:T(8,128)(2,1)}, u32[]{:S(2)}) %copy-start) | copy-done | bytes 262168
  17.7 0.0 copy-start.1
  17.7 0.7 copy-done.1
  18.4 0.3 columns.1
  18.8 6.6 %all-to-all-done.asked_ref = s32[128,1,16]{2,1,0:T(1,128)S(1)} async-done(((s32[128,1,16]{2,1,0:T(1,128)}), s32[128,1,16]{2,1,0:T(1,128)S(1)}, u32[]{:S(2)}, u32[]{:S(2)}) %all-to-all-start) | async-done | bytes 8224 | tf_op jit(solution)/shard_map/all_to_all | solution.py:241
  25.3 0.8 %gather.1 = bf16[2048,128]{1,0:T(8,128)(2,1)S(1)} custom-call(s32[128,1,16]{2,1,0:T(1,128)S(1)} %all-to-all-done.asked_ref, bf16[512,256]{1,0:T(8,128)(2,1)S(1)} %get-tuple-element.14.table_ref), custom_call_target="tpu_custom_call" | custom-call | tf_op jit(solution)/shard_map/gather/pallas_call | solution.py:60
  26.2 23.7 %all_to_all.10 = bf16[128,16,128]{2,1,0:T(8,128)(2,1)S(1)} all-to-all(bf16[128,16,128]{2,1,0:T(8,128)(2,1)S(1)} %bitcast.12), channel_id=1, replica_groups=mesh['grp'=2,'dev'=128] {'dev'}, dimensions={0} | all-to-all | bytes 1048576 | tf_op jit(solution)/shard_map/all_to_all | solution.py:246
  49.9 1.3 %lift.1 = bf16[2048,128]{1,0:T(8,128)(2,1)S(1)} custom-call(s32[2048,128]{1,0:T(8,128)S(1)} %get-tuple-element.13.refs_0_, bf16[2048,128]{1,0:T(8,128)(2,1)S(1)} %bitcast.13), custom_call_target="tpu_custom_call" | custom-call | tf_op jit(solution)/shard_map/lift/pallas_call | solution.py:108
  51.2 0.7 collective-permute-start.1
  51.8 1.5 %collective-permute-start = (bf16[2048,128]{1,0:T(8,128)(2,1)S(1)}, bf16[2048,128]{1,0:T(8,128)(2,1)S(1)}, u32[]{:S(2)}, u32[]{:S(2)}) collective-permute-start(bf16[2048,128]{1,0:T(8,128)(2,1)S(1)} %lift.1), channel_id=1, source_target_pairs={{1,2},{2,1},{3,4},{4,3},{5,6},{6,5},{7,8},{8,7},{9,10},{10,9},{11,... | collective-permute-start | bytes 1572872 | tf_op jit(solution)/shard_map/ppermute | solution.py:255
  53.3 3.5 %load.1 = (bf16[32,8,128,128]{3,2,1,0:T(8,128)(2,1)S(1)}, s32[8,32]{1,0:T(8,128)S(4)}) custom-call(bf16[32,8,128,128]{3,2,1,0:T(8,128)(2,1)} %bitcast.17, s32[8,32]{1,0:T(8,128)} %bitcast.18), custom_call_target="tpu_custom_call" | custom-call | tf_op jit(solution)/shard_map/load/pallas_call | solution.py:134
  56.9 4.4 %collective-permute-done.1 = bf16[2048,128]{1,0:T(8,128)(2,1)S(1)} collective-permute-done((bf16[2048,128]{1,0:T(8,128)(2,1)S(1)}, bf16[2048,128]{1,0:T(8,128)(2,1)S(1)}, u32[]{:S(2)}, u32[]{:S(2)}) %collective-permute-start.1) | collective-permute-done | bytes 524320 | tf_op jit(solution)/shard_map/ppermute | solution.py:256
  61.3 4.8 %collective-permute-done = bf16[2048,128]{1,0:T(8,128)(2,1)S(1)} collective-permute-done((bf16[2048,128]{1,0:T(8,128)(2,1)S(1)}, bf16[2048,128]{1,0:T(8,128)(2,1)S(1)}, u32[]{:S(2)}, u32[]{:S(2)}) %collective-permute-start) | collective-permute-done | bytes 524320 | tf_op jit(solution)/shard_map/ppermute | solution.py:255
  66.1 0.9 %first_rows.1 = (f32[1024,128]{1,0:T(8,128)S(1)}, bf16[48,128,128]{2,1,0:T(8,128)(2,1)S(1)}) custom-call(s32[8,32]{1,0:T(8,128)S(4)} %get-tuple-element.11.cols_ref, bf16[32,8,128,128]{3,2,1,0:T(8,128)(2,1)S(1)} %get-tuple-element.12.tiles_ref, bf16[16,128,128]{2,1,0:T(8,128)(2,1)S(1)} %bitcast.15, bf16[16,128,128]{2,1,0:T(8,128)(2,1)S(1)} %bitcast.11, ...), custom_call_target="tpu_custom_call" | custom-call | tf_op jit(solution)/shard_map/first_rows/pallas_call | solution.py:175
  67.0 1.0 %more_rows.3.refs_0_ = f32[1536,128]{1,0:T(8,128)S(1)} custom-call(s32[8,32]{1,0:T(8,128)S(4)} %get-tuple-element.11.cols_ref, bf16[32,8,128,128]{3,2,1,0:T(8,128)(2,1)S(1)} %get-tuple-element.12.tiles_ref, bf16[48,128,128]{2,1,0:T(8,128)(2,1)S(1)} %get-tuple-element.15.blocks_ref), custom_call_target="tpu_custom_call" | custom-call | tf_op jit(solution)/shard_map/more_rows/pallas_call | solution.py:193
  68.0 4.4 %collective-permute-start.3 = (f32[1536,128]{1,0:T(8,128)S(1)}, f32[1536,128]{1,0:T(8,128)S(1)}, u32[]{:S(2)}, u32[]{:S(2)}) collective-permute-start(f32[1536,128]{1,0:T(8,128)S(1)} %more_rows.3.refs_0_), channel_id=1, source_target_pairs={{0,128},{128,0},{1,129},{129,1},{2,130},{130,2},{3,131},{131,3},{4... | collective-permute-start | bytes 2359304 | tf_op jit(solution)/shard_map/ppermute | solution.py:265
  72.4 1.0 %more_rows.2.refs_0_ = f32[1536,128]{1,0:T(8,128)S(1)} custom-call(s32[8,32]{1,0:T(8,128)S(4)} %get-tuple-element.11.cols_ref, bf16[32,8,128,128]{3,2,1,0:T(8,128)(2,1)S(1)} %get-tuple-element.12.tiles_ref, bf16[48,128,128]{2,1,0:T(8,128)(2,1)S(1)} %get-tuple-element.15.blocks_ref), custom_call_target="tpu_custom_call" | custom-call | tf_op jit(solution)/shard_map/more_rows/pallas_call | solution.py:193
  73.3 0.1 collective-permute-start.2
  73.4 0.5 collective-permute-start.4
  73.9 2.5 %collective-permute-done.4.refs_1_ = f32[1024,128]{1,0:T(8,128)S(1)} collective-permute-done((f32[1024,128]{1,0:T(8,128)S(1)}, f32[1024,128]{1,0:T(8,128)S(1)}, u32[]{:S(2)}, u32[]{:S(2)}) %collective-permute-start.4) | collective-permute-done | bytes 524320 | tf_op jit(solution)/shard_map/ppermute | solution.py:265
  76.5 0.8 combine.3.refs_2_
  77.2 0.0 collective-permute-done.3.refs_1_
  77.2 0.8 %combine.4.refs_2_ = bf16[4096,128]{1,0:T(8,128)(2,1)} custom-call(f32[1536,128]{1,0:T(8,128)S(1)} %more_rows.3.refs_0_, f32[1536,128]{1,0:T(8,128)S(1)} %collective-permute-done.3.refs_1_, bf16[4096,128]{1,0:T(8,128)(2,1)} %combine.3.refs_2_), custom_call_target="tpu_custom_call", output_to_operand_aliasing={{}: (2, {})} | custom-call | tf_op jit(solution)/shard_map/combine/pallas_call | solution.py:221
  78.1 0.0 collective-permute-done.2.refs_1_
  78.1 0.8 %combine.5 = bf16[4096,128]{1,0:T(8,128)(2,1)} custom-call(f32[1536,128]{1,0:T(8,128)S(1)} %more_rows.2.refs_0_, f32[1536,128]{1,0:T(8,128)S(1)} %collective-permute-done.2.refs_1_, bf16[4096,128]{1,0:T(8,128)(2,1)} %combine.4.refs_2_), custom_call_target="tpu_custom_call", output_to_operand_aliasing={{}: (2, {})} | custom-call | tf_op jit(solution)/shard_map/combine/pallas_call | solution.py:221
Async XLA Ops:
  1.4 23.9 %all-to-all-start = ((s32[128,1,16]{2,1,0:T(1,128)}), s32[128,1,16]{2,1,0:T(1,128)S(1)}, u32[]{:S(2)}, u32[]{:S(2)}) async-start(s32[128,1,16]{2,1,0:T(1,128)} %bitcast.4), calls=%async_computation | async-start | bytes 131072 | tf_op jit(solution)/shard_map/all_to_all | solution.py:241
  16.8 1.0 %copy-start = (bf16[1024,128]{1,0:T(8,128)(2,1)S(1)}, bf16[1024,128]{1,0:T(8,128)(2,1)}, u32[]{:S(2)}) copy-start(bf16[1024,128]{1,0:T(8,128)(2,1)} %refs_0_.1) | copy-start | bytes 786436
  17.7 0.7 copy-start.1
  51.2 10.1 %collective-permute-start.1 = (bf16[2048,128]{1,0:T(8,128)(2,1)S(1)}, bf16[2048,128]{1,0:T(8,128)(2,1)S(1)}, u32[]{:S(2)}, u32[]{:S(2)}) collective-permute-start(bf16[2048,128]{1,0:T(8,128)(2,1)S(1)} %lift.1), channel_id=1, source_target_pairs={{0,1},{1,0},{2,3},{3,2},{4,5},{5,4},{6,7},{7,6},{8,9},{9,8},{10,11... | collective-permute-start | bytes 1572872 | tf_op jit(solution)/shard_map/ppermute | solution.py:256
  51.8 14.3 %collective-permute-start = (bf16[2048,128]{1,0:T(8,128)(2,1)S(1)}, bf16[2048,128]{1,0:T(8,128)(2,1)S(1)}, u32[]{:S(2)}, u32[]{:S(2)}) collective-permute-start(bf16[2048,128]{1,0:T(8,128)(2,1)S(1)} %lift.1), channel_id=1, source_target_pairs={{1,2},{2,1},{3,4},{4,3},{5,6},{6,5},{7,8},{8,7},{9,10},{10,9},{11,... | collective-permute-start | bytes 1572872 | tf_op jit(solution)/shard_map/ppermute | solution.py:255
  68.0 9.2 %collective-permute-start.3 = (f32[1536,128]{1,0:T(8,128)S(1)}, f32[1536,128]{1,0:T(8,128)S(1)}, u32[]{:S(2)}, u32[]{:S(2)}) collective-permute-start(f32[1536,128]{1,0:T(8,128)S(1)} %more_rows.3.refs_0_), channel_id=1, source_target_pairs={{0,128},{128,0},{1,129},{129,1},{2,130},{130,2},{3,131},{131,3},{4... | collective-permute-start | bytes 2359304 | tf_op jit(solution)/shard_map/ppermute | solution.py:265
  73.3 4.7 %collective-permute-start.2 = (f32[1536,128]{1,0:T(8,128)S(1)}, f32[1536,128]{1,0:T(8,128)S(1)}, u32[]{:S(2)}, u32[]{:S(2)}) collective-permute-start(f32[1536,128]{1,0:T(8,128)S(1)} %more_rows.2.refs_0_), channel_id=1, source_target_pairs={{0,128},{128,0},{1,129},{129,1},{2,130},{130,2},{3,131},{131,3},{4... | collective-permute-start | bytes 2359304 | tf_op jit(solution)/shard_map/ppermute | solution.py:265
  73.4 3.0 %collective-permute-start.4 = (f32[1024,128]{1,0:T(8,128)S(1)}, f32[1024,128]{1,0:T(8,128)S(1)}, u32[]{:S(2)}, u32[]{:S(2)}) collective-permute-start(f32[1024,128]{1,0:T(8,128)S(1)} %get-tuple-element.16.refs_0_), channel_id=1, source_target_pairs={{0,128},{128,0},{1,129},{129,1},{2,130},{130,2},{3,131},{131,3},{4... | collective-permute-start | bytes 1572872 | tf_op jit(solution)/shard_map/ppermute | solution.py:265

commit v6 on v5

--- a/solution.py
+++ b/solution.py
@@ -36,6 +36,46 @@
     width = table.shape[1] // 2
     found = jnp.dot(onehot, table, preferred_element_type=jnp.float32)
     return jnp.where(wanted >= depth, found[:, width:], found[:, :width])
+
+
+def start_body(
+    lists_ref, table_ref, index_ref, lists_out, table_out, index_out, lists_buffer, table_buffer, sems
+):
+    copies = [
+        pltpu.make_async_copy(lists_ref, lists_buffer, sems.at[0]),
+        pltpu.make_async_copy(table_ref, table_buffer, sems.at[1]),
+        pltpu.make_async_copy(index_ref, index_out, sems.at[2]),
+    ]
+    for copy in copies:
+        copy.start()
+    copies[0].wait()
+    slots, owners = lists_ref.shape
+    filled = jnp.concatenate([lists_buffer[...]] * (owners // slots), axis=0)
+    lists_out[...] = jnp.transpose(filled)[:, :slots]
+    copies[1].wait()
+    table_out[...] = side_by_side(table_buffer)
+    copies[2].wait()
+
+
+def start(lists, table, index):
+    rows, width = table.shape
+    return pl.pallas_call(
+        start_body,
+        out_shape=(
+            pltpu.VMEM(lists.shape[::-1], lists.dtype),
+            pltpu.VMEM((rows // 2, 2 * width), table.dtype),
+            pltpu.VMEM(index.shape, index.dtype),
+        ),
+        in_specs=[pl.BlockSpec(memory_space=pltpu.HBM)] * 3,
+        out_specs=(VMEM_SPEC,) * 3,
+        scratch_shapes=[
+            pltpu.VMEM(lists.shape, lists.dtype),
+            pltpu.VMEM(table.shape, table.dtype),
+            pltpu.SemaphoreType.DMA((3,)),
+        ],
+        compiler_params=pltpu.CompilerParams(vmem_limit_bytes=56 * 1024 * 1024),
+        name="start",
+    )(lists, table, index)
 
 
 def gather_body(asked_ref, table_ref, out_ref):
@@ -56,10 +96,9 @@
 
 
 def gather(asked, table):
-    count = asked.size
     return pl.pallas_call(
         gather_body,
-        out_shape=jax.ShapeDtypeStruct((count, table.shape[1] // 2), table.dtype),
+        out_shape=jax.ShapeDtypeStruct((asked.size, table.shape[1] // 2), table.dtype),
         in_specs=[VMEM_SPEC, VMEM_SPEC],
         out_specs=VMEM_SPEC,
         compiler_params=PARAMS,
@@ -67,52 +106,22 @@
     )(asked, table)
 
 
-def columns_body(index_ref, *refs, first):
-    out_ref = refs[-1]
-    for b in range(out_ref.shape[0] // LANES):
-        out_ref[b * LANES : (b + 1) * LANES, :] = column_of(index_ref, first + b)
-    if len(refs) == 3:
-        refs[1][...] = side_by_side(refs[0])
-
-
-def columns(index, first, count, table=None):
-    wide = jax.ShapeDtypeStruct((count * LANES, LANES), jnp.int32)
-    shapes, arrays = (wide,), (index,)
-    if table is not None:
-        rows, width = table.shape
-        shapes = (jax.ShapeDtypeStruct((rows // 2, 2 * width), table.dtype), wide)
-        arrays = (index, table)
-    return pl.pallas_call(
-        functools.partial(columns_body, first=first),
-        out_shape=shapes,
-        in_specs=[VMEM_SPEC] * len(arrays),
-        out_specs=(VMEM_SPEC,) * len(shapes),
-        compiler_params=PARAMS,
-        name="columns",
-    )(*arrays)
-
-
-def lift_body(*refs):
-    table_ref, out_ref = refs[-2:]
+def lift_body(index_ref, table_ref, out_ref):
     table = side_by_side(table_ref)
-    start = 0
-    for wanted_ref in refs[:-2]:
-        for b in range(wanted_ref.shape[0] // LANES):
-            rows = slice(b * LANES, (b + 1) * LANES)
-            value = rows_of(wanted_ref[rows, :], table, table_ref.shape[0] // 2)
-            out_ref[start : start + LANES, :] = value.astype(out_ref.dtype)
-            start += LANES
-
-
-def lift(parts, table):
+    for b in range(index_ref.shape[0]):
+        value = rows_of(column_of(index_ref, b), table, table_ref.shape[0] // 2)
+        out_ref[b * LANES : (b + 1) * LANES, :] = value.astype(out_ref.dtype)
+
+
+def lift(index, table):
     return pl.pallas_call(
         lift_body,
-        out_shape=jax.ShapeDtypeStruct((sum(p.shape[0] for p in parts), table.shape[1]), table.dtype),
-        in_specs=[VMEM_SPEC] * (len(parts) + 1),
+        out_shape=jax.ShapeDtypeStruct((index.size, table.shape[1]), table.dtype),
+        in_specs=[VMEM_SPEC, VMEM_SPEC],
         out_specs=VMEM_SPEC,
         compiler_params=PARAMS,
         name="lift",
-    )(*parts, table)
+    )(index, table)
 
 
 def load_body(tiles_ref, cols_ref, out_ref, cols_out_ref, sems, *, pieces):
@@ -235,18 +244,16 @@
     slots = req_ids.shape[3]
     width = coarse_emb.shape[1]
     row_blocks = tiles.shape[0]
-    index = fine_slot.reshape(-1, LANES)
-    half = index.shape[0] // 2
+    lists, table, index = start(req_ids[0, 0].T, coarse_emb, fine_slot.reshape(-1, LANES))
     tiles, cols = load(tiles[:, 0], tile_cols[:, 0].T)
     asked = lax.all_to_all(
-        req_ids.reshape(devices, 1, slots), "dev", split_axis=0, concat_axis=0, tiled=True
-    )
-    table, first = columns(index, 0, 2 * half, coarse_emb)
+        lists.reshape(devices, 1, slots), "dev", split_axis=0, concat_axis=0, tiled=True
+    )
     wanted = gather(asked, table)
     received = lax.all_to_all(
         wanted.reshape(devices, slots, width), "dev", split_axis=0, concat_axis=0, tiled=True
     )
-    lifted = lift((first,), received.reshape(devices * slots, width))
+    lifted = lift(index, received.reshape(devices * slots, width))
     inner = [(i, i ^ 1) for i in range(devices)]
     outer = []
     for g in range(groups):

time: 79.2 us -> 78.6 us (level)
  blocking collectives: 23.7 us -> 47.5 us
  starting transfers between devices: 22.5 us -> 7.14 us
  waiting for transfers between devices: 18.4 us -> 11.8 us
  local copies, waits for them, and re-layouts: 3.07 us -> 0 us
    all_to_all x0 -> x1, blocking collectives: none -> 23.8 us  [per_device(): lax.all_to_all(lists.reshape(devices, 1, slots), 'dev', split_axis=0, con...]
    all_to_all x1 -> x0, starting transfers between devices: 15.3 us -> none  [per_device(): lax.all_to_all(req_ids.reshape(devices, 1, slots), 'dev', split_axis=0, c...]
    all_to_all x1 -> x0, waiting for transfers between devices: 6.57 us -> none  [per_device(): lax.all_to_all(req_ids.reshape(devices, 1, slots), 'dev', split_axis=0, c...]
    unnamed x5 -> x0, local copies, waits for them, and re-layouts: 3.07 us -> none
  transfers between devices with their start and end apart: 6 -> 5, of which waited for: 4 -> 3; matrix products, arithmetic and copies ran while one was open for 0% -> 0% of each run, Pallas kernels for 8% -> 8%
where the time goes in v6:
time: 78.6 us; the launch traced here: 78.4 us
  blocking collectives  47.5 us (60%)
  Pallas kernels  11.9 us (15%)
  waiting for transfers between devices  11.8 us (15%)
  starting transfers between devices  7.14 us (9%)
    all_to_all x1, blocking collectives, per_device(): lax.all_to_all(lists.reshape(devices, 1, slots), 'dev', split_axis=0, con...  23.8 us
    all_to_all x1, blocking collectives, per_device(): lax.all_to_all(wanted.reshape(devices, slots, width), 'dev', split_axis=0...  23.7 us
    ppermute x3, starting transfers between devices, per_device(): parts.append((mine, lax.ppermute(mine, 'grp', [(0, 1), (1, 0)])))  4.95 us
    ppermute x1, waiting for transfers between devices, per_device(): lax.ppermute(lifted, ('grp', 'dev'), outer).reshape(-1, LANES, width)  4.85 us
    ppermute x1, waiting for transfers between devices, per_device(): from_inner = lax.ppermute(lifted, 'dev', inner).reshape(-1, LANES, width)  4.41 us
    pallas_call x1, Pallas kernels, load(): pl.pallas_call(functools.partial(load_body, pieces=4), out_shape=(pltpu.V...  3.52 us
    ppermute x3, waiting for transfers between devices, per_device(): parts.append((mine, lax.ppermute(mine, 'grp', [(0, 1), (1, 0)])))  2.53 us
    pallas_call x3, Pallas kernels, combine(): pl.pallas_call(functools.partial(combine_body, first=first), out_shape=ja...  2.41 us
  transfers between devices with their start and end apart: 5, of which 3 were waited for; matrix products, arithmetic and copies ran while one was open for 0% of the time, Pallas kernels for 8%

profile of v6, /device:TPU:7, one launch (start us, length us, event | category | flops | bytes accessed | tf_op | source)
XLA Modules:
  0.0 78.4 jit_solution(15575255190251289834)
XLA Ops:
  0.0 1.0 %start.1 = (s32[128,16]{1,0:T(8,128)S(1)}, bf16[512,256]{1,0:T(8,128)(2,1)S(1)}, s32[16,128]{1,0:T(8,128)S(1)}) custom-call(s32[16,128]{1,0:T(8,128)} %bitcast.21, bf16[1024,128]{1,0:T(8,128)(2,1)} %table_ref.1, s32[16,128]{1,0:T(8,128)} %bitcast.22), custom_call_target="tpu_custom_call" | custom-call | tf_op jit(solution)/shard_map/start/pallas_call | solution.py:62
  1.0 23.8 %all_to_all.10.asked_ref = s32[128,1,16]{2,1,0:T(1,128)S(1)} all-to-all(s32[128,1,16]{2,1,0:T(1,128)S(1)} %bitcast.19), channel_id=1, replica_groups=mesh['grp'=2,'dev'=128] {'dev'}, dimensions={0} | all-to-all | bytes 16384 | tf_op jit(solution)/shard_map/all_to_all | solution.py:249
  24.8 0.8 %gather.1 = bf16[2048,128]{1,0:T(8,128)(2,1)S(1)} custom-call(s32[128,1,16]{2,1,0:T(1,128)S(1)} %all_to_all.10.asked_ref, bf16[512,256]{1,0:T(8,128)(2,1)S(1)} %get-tuple-element.16.table_ref), custom_call_target="tpu_custom_call" | custom-call | tf_op jit(solution)/shard_map/gather/pallas_call | solution.py:99
  25.6 23.7 %all_to_all.11 = bf16[128,16,128]{2,1,0:T(8,128)(2,1)S(1)} all-to-all(bf16[128,16,128]{2,1,0:T(8,128)(2,1)S(1)} %bitcast.16), channel_id=1, replica_groups=mesh['grp'=2,'dev'=128] {'dev'}, dimensions={0} | all-to-all | bytes 1048576 | tf_op jit(solution)/shard_map/all_to_all | solution.py:253
  49.4 1.3 %lift.1 = bf16[2048,128]{1,0:T(8,128)(2,1)S(1)} custom-call(s32[16,128]{1,0:T(8,128)S(1)} %get-tuple-element.14.index_ref, bf16[2048,128]{1,0:T(8,128)(2,1)S(1)} %bitcast.15), custom_call_target="tpu_custom_call" | custom-call | tf_op jit(solution)/shard_map/lift/pallas_call | solution.py:117
  50.7 0.7 collective-permute-start.1
  51.4 1.5 %collective-permute-start = (bf16[2048,128]{1,0:T(8,128)(2,1)S(1)}, bf16[2048,128]{1,0:T(8,128)(2,1)S(1)}, u32[]{:S(2)}, u32[]{:S(2)}) collective-permute-start(bf16[2048,128]{1,0:T(8,128)(2,1)S(1)} %lift.1), channel_id=1, source_target_pairs={{1,2},{2,1},{3,4},{4,3},{5,6},{6,5},{7,8},{8,7},{9,10},{10,9},{11,... | collective-permute-start | bytes 1572872 | tf_op jit(solution)/shard_map/ppermute | solution.py:262
  52.9 3.5 %load.1 = (bf16[32,8,128,128]{3,2,1,0:T(8,128)(2,1)S(1)}, s32[8,32]{1,0:T(8,128)S(4)}) custom-call(bf16[32,8,128,128]{3,2,1,0:T(8,128)(2,1)} %bitcast.20, s32[8,32]{1,0:T(8,128)} %bitcast.23), custom_call_target="tpu_custom_call" | custom-call | tf_op jit(solution)/shard_map/load/pallas_call | solution.py:143
  56.4 4.4 %collective-permute-done.1 = bf16[2048,128]{1,0:T(8,128)(2,1)S(1)} collective-permute-done((bf16[2048,128]{1,0:T(8,128)(2,1)S(1)}, bf16[2048,128]{1,0:T(8,128)(2,1)S(1)}, u32[]{:S(2)}, u32[]{:S(2)}) %collective-permute-start.1) | collective-permute-done | bytes 524320 | tf_op jit(solution)/shard_map/ppermute | solution.py:263
  60.8 4.8 %collective-permute-done = bf16[2048,128]{1,0:T(8,128)(2,1)S(1)} collective-permute-done((bf16[2048,128]{1,0:T(8,128)(2,1)S(1)}, bf16[2048,128]{1,0:T(8,128)(2,1)S(1)}, u32[]{:S(2)}, u32[]{:S(2)}) %collective-permute-start) | collective-permute-done | bytes 524320 | tf_op jit(solution)/shard_map/ppermute | solution.py:262
  65.7 0.9 %first_rows.1 = (f32[1024,128]{1,0:T(8,128)S(1)}, bf16[48,128,128]{2,1,0:T(8,128)(2,1)S(1)}) custom-call(s32[8,32]{1,0:T(8,128)S(4)} %get-tuple-element.12.cols_ref, bf16[32,8,128,128]{3,2,1,0:T(8,128)(2,1)S(1)} %get-tuple-element.13.tiles_ref, bf16[16,128,128]{2,1,0:T(8,128)(2,1)S(1)} %bitcast.18, bf16[16,128,128]{2,1,0:T(8,128)(2,1)S(1)} %bitcast.14, ...), custom_call_target="tpu_custom_call" | custom-call | tf_op jit(solution)/shard_map/first_rows/pallas_call | solution.py:184
  66.5 1.0 %more_rows.3.refs_0_ = f32[1536,128]{1,0:T(8,128)S(1)} custom-call(s32[8,32]{1,0:T(8,128)S(4)} %get-tuple-element.12.cols_ref, bf16[32,8,128,128]{3,2,1,0:T(8,128)(2,1)S(1)} %get-tuple-element.13.tiles_ref, bf16[48,128,128]{2,1,0:T(8,128)(2,1)S(1)} %get-tuple-element.17.blocks_ref), custom_call_target="tpu_custom_call" | custom-call | tf_op jit(solution)/shard_map/more_rows/pallas_call | solution.py:202
  67.5 4.4 %collective-permute-start.3 = (f32[1536,128]{1,0:T(8,128)S(1)}, f32[1536,128]{1,0:T(8,128)S(1)}, u32[]{:S(2)}, u32[]{:S(2)}) collective-permute-start(f32[1536,128]{1,0:T(8,128)S(1)} %more_rows.3.refs_0_), channel_id=1, source_target_pairs={{0,128},{128,0},{1,129},{129,1},{2,130},{130,2},{3,131},{131,3},{4... | collective-permute-start | bytes 2359304 | tf_op jit(solution)/shard_map/ppermute | solution.py:272
  71.9 1.0 %more_rows.2.refs_0_ = f32[1536,128]{1,0:T(8,128)S(1)} custom-call(s32[8,32]{1,0:T(8,128)S(4)} %get-tuple-element.12.cols_ref, bf16[32,8,128,128]{3,2,1,0:T(8,128)(2,1)S(1)} %get-tuple-element.13.tiles_ref, bf16[48,128,128]{2,1,0:T(8,128)(2,1)S(1)} %get-tuple-element.17.blocks_ref), custom_call_target="tpu_custom_call" | custom-call | tf_op jit(solution)/shard_map/more_rows/pallas_call | solution.py:202
  72.9 0.1 collective-permute-start.2
  73.0 0.5 collective-permute-start.4
  73.5 2.5 %collective-permute-done.4.refs_1_ = f32[1024,128]{1,0:T(8,128)S(1)} collective-permute-done((f32[1024,128]{1,0:T(8,128)S(1)}, f32[1024,128]{1,0:T(8,128)S(1)}, u32[]{:S(2)}, u32[]{:S(2)}) %collective-permute-start.4) | collective-permute-done | bytes 524320 | tf_op jit(solution)/shard_map/ppermute | solution.py:272
  76.0 0.8 combine.3.refs_2_
  76.8 0.0 collective-permute-done.3.refs_1_
  76.8 0.8 %combine.4.refs_2_ = bf16[4096,128]{1,0:T(8,128)(2,1)} custom-call(f32[1536,128]{1,0:T(8,128)S(1)} %more_rows.3.refs_0_, f32[1536,128]{1,0:T(8,128)S(1)} %collective-permute-done.3.refs_1_, bf16[4096,128]{1,0:T(8,128)(2,1)} %combine.3.refs_2_), custom_call_target="tpu_custom_call", output_to_operand_aliasing={{}: (2, {})} | custom-call | tf_op jit(solution)/shard_map/combine/pallas_call | solution.py:230
  77.6 0.0 collective-permute-done.2.refs_1_
  77.6 0.8 %combine.5 = bf16[4096,128]{1,0:T(8,128)(2,1)} custom-call(f32[1536,128]{1,0:T(8,128)S(1)} %more_rows.2.refs_0_, f32[1536,128]{1,0:T(8,128)S(1)} %collective-permute-done.2.refs_1_, bf16[4096,128]{1,0:T(8,128)(2,1)} %combine.4.refs_2_), custom_call_target="tpu_custom_call", output_to_operand_aliasing={{}: (2, {})} | custom-call | tf_op jit(solution)/shard_map/combine/pallas_call | solution.py:230
Async XLA Ops:
  50.7 10.1 %collective-permute-start.1 = (bf16[2048,128]{1,0:T(8,128)(2,1)S(1)}, bf16[2048,128]{1,0:T(8,128)(2,1)S(1)}, u32[]{:S(2)}, u32[]{:S(2)}) collective-permute-start(bf16[2048,128]{1,0:T(8,128)(2,1)S(1)} %lift.1), channel_id=1, source_target_pairs={{0,1},{1,0},{2,3},{3,2},{4,5},{5,4},{6,7},{7,6},{8,9},{9,8},{10,11... | collective-permute-start | bytes 1572872 | tf_op jit(solution)/shard_map/ppermute | solution.py:263
  51.4 14.3 %collective-permute-start = (bf16[2048,128]{1,0:T(8,128)(2,1)S(1)}, bf16[2048,128]{1,0:T(8,128)(2,1)S(1)}, u32[]{:S(2)}, u32[]{:S(2)}) collective-permute-start(bf16[2048,128]{1,0:T(8,128)(2,1)S(1)} %lift.1), channel_id=1, source_target_pairs={{1,2},{2,1},{3,4},{4,3},{5,6},{6,5},{7,8},{8,7},{9,10},{10,9},{11,... | collective-permute-start | bytes 1572872 | tf_op jit(solution)/shard_map/ppermute | solution.py:262
  67.5 9.2 %collective-permute-start.3 = (f32[1536,128]{1,0:T(8,128)S(1)}, f32[1536,128]{1,0:T(8,128)S(1)}, u32[]{:S(2)}, u32[]{:S(2)}) collective-permute-start(f32[1536,128]{1,0:T(8,128)S(1)} %more_rows.3.refs_0_), channel_id=1, source_target_pairs={{0,128},{128,0},{1,129},{129,1},{2,130},{130,2},{3,131},{131,3},{4... | collective-permute-start | bytes 2359304 | tf_op jit(solution)/shard_map/ppermute | solution.py:272
  72.9 4.7 %collective-permute-start.2 = (f32[1536,128]{1,0:T(8,128)S(1)}, f32[1536,128]{1,0:T(8,128)S(1)}, u32[]{:S(2)}, u32[]{:S(2)}) collective-permute-start(f32[1536,128]{1,0:T(8,128)S(1)} %more_rows.2.refs_0_), channel_id=1, source_target_pairs={{0,128},{128,0},{1,129},{129,1},{2,130},{130,2},{3,131},{131,3},{4... | collective-permute-start | bytes 2359304 | tf_op jit(solution)/shard_map/ppermute | solution.py:272
  73.0 3.0 %collective-permute-start.4 = (f32[1024,128]{1,0:T(8,128)S(1)}, f32[1024,128]{1,0:T(8,128)S(1)}, u32[]{:S(2)}, u32[]{:S(2)}) collective-permute-start(f32[1024,128]{1,0:T(8,128)S(1)} %get-tuple-element.18.refs_0_), channel_id=1, source_target_pairs={{0,128},{128,0},{1,129},{129,1},{2,130},{130,2},{3,131},{131,3},{4... | collective-permute-start | bytes 1572872 | tf_op jit(solution)/shard_map/ppermute | solution.py:272

commit v7 on v6

--- a/solution.py
+++ b/solution.py
@@ -12,7 +12,8 @@
 VMEM_SPEC = pl.BlockSpec(memory_space=pltpu.VMEM)
 SMEM_SPEC = pl.BlockSpec(memory_space=pltpu.SMEM)
 PARAMS = pltpu.CompilerParams(vmem_limit_bytes=16 * 1024 * 1024)
-CHUNKS = (8, 12, 12)
+CHUNKS = (8, 16, 8)
+PIECES = 4
 
 
 def column_of(index_ref, b):
@@ -210,16 +211,18 @@
 
 
 def combine_body(*refs, first):
-    out_ref, buffer, sem = refs[-3:]
-    pairs = (len(refs) - 3) // 2
-    start = 0
-    for mine_ref, theirs_ref in zip(refs[: 2 * pairs : 2], refs[1 : 2 * pairs : 2]):
-        rows = mine_ref.shape[0]
-        buffer[start : start + rows, :] = (mine_ref[...] + theirs_ref[...]).astype(buffer.dtype)
-        start += rows
-    copy = pltpu.make_async_copy(buffer, out_ref.at[pl.ds(first, start)], sem)
-    copy.start()
-    copy.wait()
+    out_ref, buffer, sems = refs[-3:]
+    mine_ref, theirs_ref = refs[:2]
+    each = buffer.shape[0] // PIECES
+    copies = []
+    for p in range(PIECES):
+        rows = slice(p * each, (p + 1) * each)
+        buffer[rows, :] = (mine_ref[rows, :] + theirs_ref[rows, :]).astype(buffer.dtype)
+        target = out_ref.at[pl.ds(first + p * each, each)]
+        copies.append(pltpu.make_async_copy(buffer.at[pl.ds(p * each, each)], target, sems.at[p]))
+        copies[-1].start()
+    for copy in copies:
+        copy.wait()
 
 
 def combine(pairs, out, rows, first, dtype):
@@ -233,7 +236,7 @@
         in_specs=[VMEM_SPEC] * len(parts) + [anywhere] * len(before),
         out_specs=anywhere,
         input_output_aliases={len(parts): 0} if before else {},
-        scratch_shapes=[pltpu.VMEM((count, width), dtype), pltpu.SemaphoreType.DMA],
+        scratch_shapes=[pltpu.VMEM((count, width), dtype), pltpu.SemaphoreType.DMA((PIECES,))],
         compiler_params=PARAMS,
         name="combine",
     )(*parts, *before)

time: 78.6 us -> 77.8 us (0.990)
  waiting for transfers between devices: 11.8 us -> 11 us
    ppermute x3, waiting for transfers between devices: 2.53 us -> 1.74 us  [per_device(): parts.append((mine, lax.ppermute(mine, 'grp', [(0, 1), (1, 0)])))]
  transfers between devices with their start and end apart: 5 -> 5, of which waited for: 3 -> 3; matrix products, arithmetic and copies ran while one was open for 0% -> 0% of each run, Pallas kernels for 8% -> 7%
where the time goes in v7:
time: 77.8 us; the launch traced here: 77.6 us
  blocking collectives  47.5 us (61%)
  Pallas kernels  11.8 us (15%)
  waiting for transfers between devices  11 us (14%)
  starting transfers between devices  7.13 us (9%)
    all_to_all x1, blocking collectives, per_device(): lax.all_to_all(lists.reshape(devices, 1, slots), 'dev', split_axis=0, con...  23.8 us
    all_to_all x1, blocking collectives, per_device(): lax.all_to_all(wanted.reshape(devices, slots, width), 'dev', split_axis=0...  23.7 us
    ppermute x3, starting transfers between devices, per_device(): parts.append((mine, lax.ppermute(mine, 'grp', [(0, 1), (1, 0)])))  4.95 us
    ppermute x1, waiting for transfers between devices, per_device(): lax.ppermute(lifted, ('grp', 'dev'), outer).reshape(-1, LANES, width)  4.85 us
    ppermute x1, waiting for transfers between devices, per_device(): from_inner = lax.ppermute(lifted, 'dev', inner).reshape(-1, LANES, width)  4.41 us
    pallas_call x1, Pallas kernels, load(): pl.pallas_call(functools.partial(load_body, pieces=4), out_shape=(pltpu.V...  3.52 us
    pallas_call x3, Pallas kernels, combine(): pl.pallas_call(functools.partial(combine_body, first=first), out_shape=ja...  2.33 us
    pallas_call x2, Pallas kernels, more_rows(): pl.pallas_call(functools.partial(more_body, base=base), out_shape=jax.Sha...  1.96 us
  transfers between devices with their start and end apart: 5, of which 3 were waited for; matrix products, arithmetic and copies ran while one was open for 0% of the time, Pallas kernels for 7%

profile of v7, /device:TPU:7, one launch (start us, length us, event | category | flops | bytes accessed | tf_op | source)
XLA Modules:
  0.0 77.6 jit_solution(6473565016451341975)
XLA Ops:
  0.0 1.0 %start.1 = (s32[128,16]{1,0:T(8,128)S(1)}, bf16[512,256]{1,0:T(8,128)(2,1)S(1)}, s32[16,128]{1,0:T(8,128)S(1)}) custom-call(s32[16,128]{1,0:T(8,128)} %bitcast.21, bf16[1024,128]{1,0:T(8,128)(2,1)} %table_ref.1, s32[16,128]{1,0:T(8,128)} %bitcast.22), custom_call_target="tpu_custom_call" | custom-call | tf_op jit(solution)/shard_map/start/pallas_call | solution.py:63
  1.0 23.8 %all_to_all.10.asked_ref = s32[128,1,16]{2,1,0:T(1,128)S(1)} all-to-all(s32[128,1,16]{2,1,0:T(1,128)S(1)} %bitcast.19), channel_id=1, replica_groups=mesh['grp'=2,'dev'=128] {'dev'}, dimensions={0} | all-to-all | bytes 16384 | tf_op jit(solution)/shard_map/all_to_all | solution.py:252
  24.8 0.8 %gather.1 = bf16[2048,128]{1,0:T(8,128)(2,1)S(1)} custom-call(s32[128,1,16]{2,1,0:T(1,128)S(1)} %all_to_all.10.asked_ref, bf16[512,256]{1,0:T(8,128)(2,1)S(1)} %get-tuple-element.16.table_ref), custom_call_target="tpu_custom_call" | custom-call | tf_op jit(solution)/shard_map/gather/pallas_call | solution.py:100
  25.6 23.7 %all_to_all.11 = bf16[128,16,128]{2,1,0:T(8,128)(2,1)S(1)} all-to-all(bf16[128,16,128]{2,1,0:T(8,128)(2,1)S(1)} %bitcast.16), channel_id=1, replica_groups=mesh['grp'=2,'dev'=128] {'dev'}, dimensions={0} | all-to-all | bytes 1048576 | tf_op jit(solution)/shard_map/all_to_all | solution.py:256
  49.4 1.3 %lift.1 = bf16[2048,128]{1,0:T(8,128)(2,1)S(1)} custom-call(s32[16,128]{1,0:T(8,128)S(1)} %get-tuple-element.14.index_ref, bf16[2048,128]{1,0:T(8,128)(2,1)S(1)} %bitcast.15), custom_call_target="tpu_custom_call" | custom-call | tf_op jit(solution)/shard_map/lift/pallas_call | solution.py:118
  50.7 0.7 collective-permute-start.1
  51.4 1.5 %collective-permute-start = (bf16[2048,128]{1,0:T(8,128)(2,1)S(1)}, bf16[2048,128]{1,0:T(8,128)(2,1)S(1)}, u32[]{:S(2)}, u32[]{:S(2)}) collective-permute-start(bf16[2048,128]{1,0:T(8,128)(2,1)S(1)} %lift.1), channel_id=1, source_target_pairs={{1,2},{2,1},{3,4},{4,3},{5,6},{6,5},{7,8},{8,7},{9,10},{10,9},{11,... | collective-permute-start | bytes 1572872 | tf_op jit(solution)/shard_map/ppermute | solution.py:265
  52.9 3.5 %load.1 = (bf16[32,8,128,128]{3,2,1,0:T(8,128)(2,1)S(1)}, s32[8,32]{1,0:T(8,128)S(4)}) custom-call(bf16[32,8,128,128]{3,2,1,0:T(8,128)(2,1)} %bitcast.20, s32[8,32]{1,0:T(8,128)} %bitcast.23), custom_call_target="tpu_custom_call" | custom-call | tf_op jit(solution)/shard_map/load/pallas_call | solution.py:144
  56.4 4.4 %collective-permute-done.1 = bf16[2048,128]{1,0:T(8,128)(2,1)S(1)} collective-permute-done((bf16[2048,128]{1,0:T(8,128)(2,1)S(1)}, bf16[2048,128]{1,0:T(8,128)(2,1)S(1)}, u32[]{:S(2)}, u32[]{:S(2)}) %collective-permute-start.1) | collective-permute-done | bytes 524320 | tf_op jit(solution)/shard_map/ppermute | solution.py:266
  60.8 4.8 %collective-permute-done = bf16[2048,128]{1,0:T(8,128)(2,1)S(1)} collective-permute-done((bf16[2048,128]{1,0:T(8,128)(2,1)S(1)}, bf16[2048,128]{1,0:T(8,128)(2,1)S(1)}, u32[]{:S(2)}, u32[]{:S(2)}) %collective-permute-start) | collective-permute-done | bytes 524320 | tf_op jit(solution)/shard_map/ppermute | solution.py:265
  65.7 0.9 %first_rows.1 = (f32[1024,128]{1,0:T(8,128)S(1)}, bf16[48,128,128]{2,1,0:T(8,128)(2,1)S(1)}) custom-call(s32[8,32]{1,0:T(8,128)S(4)} %get-tuple-element.12.cols_ref, bf16[32,8,128,128]{3,2,1,0:T(8,128)(2,1)S(1)} %get-tuple-element.13.tiles_ref, bf16[16,128,128]{2,1,0:T(8,128)(2,1)S(1)} %bitcast.18, bf16[16,128,128]{2,1,0:T(8,128)(2,1)S(1)} %bitcast.14, ...), custom_call_target="tpu_custom_call" | custom-call | tf_op jit(solution)/shard_map/first_rows/pallas_call | solution.py:185
  66.5 1.3 %more_rows.3.refs_0_ = f32[2048,128]{1,0:T(8,128)S(1)} custom-call(s32[8,32]{1,0:T(8,128)S(4)} %get-tuple-element.12.cols_ref, bf16[32,8,128,128]{3,2,1,0:T(8,128)(2,1)S(1)} %get-tuple-element.13.tiles_ref, bf16[48,128,128]{2,1,0:T(8,128)(2,1)S(1)} %get-tuple-element.17.blocks_ref), custom_call_target="tpu_custom_call" | custom-call | tf_op jit(solution)/shard_map/more_rows/pallas_call | solution.py:203
  67.8 4.4 %collective-permute-start.3 = (f32[2048,128]{1,0:T(8,128)S(1)}, f32[2048,128]{1,0:T(8,128)S(1)}, u32[]{:S(2)}, u32[]{:S(2)}) collective-permute-start(f32[2048,128]{1,0:T(8,128)S(1)} %more_rows.3.refs_0_), channel_id=1, source_target_pairs={{0,128},{128,0},{1,129},{129,1},{2,130},{130,2},{3,131},{131,3},{4... | collective-permute-start | bytes 3145736 | tf_op jit(solution)/shard_map/ppermute | solution.py:275
  72.2 0.1 collective-permute-start.4
  72.3 0.7 more_rows.2.refs_0_
  73.0 0.5 collective-permute-start.2
  73.5 1.7 %collective-permute-done.4.refs_1_ = f32[1024,128]{1,0:T(8,128)S(1)} collective-permute-done((f32[1024,128]{1,0:T(8,128)S(1)}, f32[1024,128]{1,0:T(8,128)S(1)}, u32[]{:S(2)}, u32[]{:S(2)}) %collective-permute-start.4) | collective-permute-done | bytes 524320 | tf_op jit(solution)/shard_map/ppermute | solution.py:275
  75.2 0.7 combine.3.refs_2_
  75.9 0.0 collective-permute-done.3.refs_1_
  76.0 0.8 %combine.4.refs_2_ = bf16[4096,128]{1,0:T(8,128)(2,1)} custom-call(f32[2048,128]{1,0:T(8,128)S(1)} %more_rows.3.refs_0_, f32[2048,128]{1,0:T(8,128)S(1)} %collective-permute-done.3.refs_1_, bf16[4096,128]{1,0:T(8,128)(2,1)} %combine.3.refs_2_), custom_call_target="tpu_custom_call", output_to_operand_aliasing={{}: (2, {})} | custom-call | tf_op jit(solution)/shard_map/combine/pallas_call | solution.py:233
  76.8 0.0 collective-permute-done.2.refs_1_
  76.8 0.7 combine.5
Async XLA Ops:
  50.7 10.1 %collective-permute-start.1 = (bf16[2048,128]{1,0:T(8,128)(2,1)S(1)}, bf16[2048,128]{1,0:T(8,128)(2,1)S(1)}, u32[]{:S(2)}, u32[]{:S(2)}) collective-permute-start(bf16[2048,128]{1,0:T(8,128)(2,1)S(1)} %lift.1), channel_id=1, source_target_pairs={{0,1},{1,0},{2,3},{3,2},{4,5},{5,4},{6,7},{7,6},{8,9},{9,8},{10,11... | collective-permute-start | bytes 1572872 | tf_op jit(solution)/shard_map/ppermute | solution.py:266
  51.4 14.3 %collective-permute-start = (bf16[2048,128]{1,0:T(8,128)(2,1)S(1)}, bf16[2048,128]{1,0:T(8,128)(2,1)S(1)}, u32[]{:S(2)}, u32[]{:S(2)}) collective-permute-start(bf16[2048,128]{1,0:T(8,128)(2,1)S(1)} %lift.1), channel_id=1, source_target_pairs={{1,2},{2,1},{3,4},{4,3},{5,6},{6,5},{7,8},{8,7},{9,10},{10,9},{11,... | collective-permute-start | bytes 1572872 | tf_op jit(solution)/shard_map/ppermute | solution.py:265
  67.8 8.1 %collective-permute-start.3 = (f32[2048,128]{1,0:T(8,128)S(1)}, f32[2048,128]{1,0:T(8,128)S(1)}, u32[]{:S(2)}, u32[]{:S(2)}) collective-permute-start(f32[2048,128]{1,0:T(8,128)S(1)} %more_rows.3.refs_0_), channel_id=1, source_target_pairs={{0,128},{128,0},{1,129},{129,1},{2,130},{130,2},{3,131},{131,3},{4... | collective-permute-start | bytes 3145736 | tf_op jit(solution)/shard_map/ppermute | solution.py:275
  72.2 3.0 %collective-permute-start.4 = (f32[1024,128]{1,0:T(8,128)S(1)}, f32[1024,128]{1,0:T(8,128)S(1)}, u32[]{:S(2)}, u32[]{:S(2)}) collective-permute-start(f32[1024,128]{1,0:T(8,128)S(1)} %get-tuple-element.18.refs_0_), channel_id=1, source_target_pairs={{0,128},{128,0},{1,129},{129,1},{2,130},{130,2},{3,131},{131,3},{4... | collective-permute-start | bytes 1572872 | tf_op jit(solution)/shard_map/ppermute | solution.py:275
  73.0 3.8 %collective-permute-start.2 = (f32[1024,128]{1,0:T(8,128)S(1)}, f32[1024,128]{1,0:T(8,128)S(1)}, u32[]{:S(2)}, u32[]{:S(2)}) collective-permute-start(f32[1024,128]{1,0:T(8,128)S(1)} %more_rows.2.refs_0_), channel_id=1, source_target_pairs={{0,128},{128,0},{1,129},{129,1},{2,130},{130,2},{3,131},{131,3},{4... | collective-permute-start | bytes 1572872 | tf_op jit(solution)/shard_map/ppermute | solution.py:275
